TPU v7x, 128 devices: a whole 4x4x4 slice. The times are simulated.
128 devices in a mesh: dp: 4 (over y), seq: 32 (over z, x, core).
Axes of the slice: x: 4, y: 4, z: 4, core: 2. Of those that a mesh axis runs over, the one named last changes fastest.
Arguments:
- queries: bfloat16 [4, 32768, 2048], P('dp', 'seq'), may hold values from -420 to 420
- keys: bfloat16 [4, 32768, 2048], P('dp', 'seq'), may hold values from -24 to 24
- values: bfloat16 [4, 32768, 2048], P('dp', 'seq'), may hold values from -12 to 12
- codes: int32 [4, 16, 32768], P('dp', None, 'seq'), may hold values from 0 to 511
- starts: int32 [4, 64], P('dp', 'seq'), may hold values from 0 to 1
- old_centroids: float32 [16, 512, 128], replicated, may hold values from -6 to 6
- old_counts: float32 [16, 512], replicated, may hold values from 4 to 64
Outputs:
- mixed: bfloat16 [4, 32768, 2048], P('dp', 'seq')
- codebook: float32 [16, 512, 128], P(None, 'dp')
All inputs are finite; a program needn't handle non-finite values.
Results may differ from a plain program's by a relative error of at most 0.0034.
Values sent between devices are 32-bit elements; how exact they have to be, the bound alone decides.
A program may use at most 384 MiB of HBM per device.

v0:
```python
import jax
import jax.numpy as jnp
from jax import lax
from jax.sharding import PartitionSpec as P

HEADS = 16
HEAD_DIM = 128
CODES = 512
BLOCK = 512
TOK_DEV = 1024


RETAIN = 0.9
NEGATIVE = -1e30


def prefix(part, axis, combine, identity):
    place = lax.axis_index(axis)
    gathered = jax.tree.map(lambda a: lax.all_gather(a, axis), part)
    state = jax.tree.map(lambda a, e: jnp.zeros_like(a) + jnp.asarray(e, a.dtype), part, identity)

    def one(hop, state):
        return combine(
            state, jax.tree.map(lambda a: lax.dynamic_index_in_dim(a, hop, 0, False), gathered)
        )

    return lax.fori_loop(0, place, one, state)


def one_hot_rows(code_block):
    return (code_block[:, :, None] == lax.iota(jnp.int32, CODES)[None, None, :]).astype(
        jnp.bfloat16
    )


def refresh_codes(sums, counts, centroids, previous):
    return (RETAIN * previous[..., None] * centroids + (1.0 - RETAIN) * sums) / (
        RETAIN * previous + (1.0 - RETAIN) * counts
    )[..., None]


def join_segments(earlier, later):
    survive = 1.0 - later[2][0]
    return (
        later[0] + survive * earlier[0],
        later[1] + survive * earlier[1],
        jnp.maximum(earlier[2], later[2]),
    )


def shards(queries, keys, values, codes, starts, old_centroids, old_counts):
    blocks_here = TOK_DEV // BLOCK
    flags = starts[0].astype(jnp.float32)
    key_sums = jnp.zeros((HEADS, CODES, HEAD_DIM), jnp.float32)
    code_counts = jnp.zeros((HEADS, CODES), jnp.float32)
    hot_list = []
    value_sums = []
    value_counts = []
    for block_id in range(blocks_here):
        offset = block_id * BLOCK
        hot_table = one_hot_rows(codes[0, :, offset : offset + BLOCK])
        key_part = keys[0, offset : offset + BLOCK].reshape(BLOCK, HEADS, HEAD_DIM)
        value_part = values[0, offset : offset + BLOCK].reshape(BLOCK, HEADS, HEAD_DIM)
        key_sums = key_sums + jnp.einsum(
            "hts,thd->hsd", hot_table, key_part, preferred_element_type=jnp.float32
        )
        counted = jnp.sum(hot_table, axis=1, dtype=jnp.float32)
        code_counts = code_counts + counted
        value_sums.append(
            jnp.einsum("hts,thd->hsd", hot_table, value_part, preferred_element_type=jnp.float32)
        )
        value_counts.append(counted)
        hot_list.append(hot_table)
    total_keys, total_counts = lax.psum((key_sums, code_counts), ("dp", "seq"))
    codebook = refresh_codes(total_keys, total_counts, old_centroids, old_counts)
    code_share = CODES // lax.axis_size("dp")
    codebook_out = lax.dynamic_slice_in_dim(
        codebook, lax.axis_index("dp") * code_share, code_share, 1
    )
    tail_sums = jnp.zeros((HEADS, CODES, HEAD_DIM), jnp.float32)
    tail_counts = jnp.zeros((HEADS, CODES), jnp.float32)
    flag_any = jnp.zeros((1,), jnp.float32)
    for block_id in range(blocks_here):
        survive = 1.0 - flags[block_id]
        tail_sums = survive * tail_sums + value_sums[block_id]
        tail_counts = survive * tail_counts + value_counts[block_id]
        flag_any = jnp.maximum(flag_any, flags[block_id])
    identity = (
        jnp.zeros_like(tail_sums),
        jnp.zeros_like(tail_counts),
        jnp.zeros((1,), jnp.float32),
    )
    enter_sums, enter_counts, ignored_flag = prefix(
        (tail_sums, tail_counts, flag_any), "seq", join_segments, identity
    )
    codebook_half = codebook.astype(jnp.bfloat16)
    score_scale = HEAD_DIM ** (-0.5)
    positions = lax.iota(jnp.int32, BLOCK)
    causal = positions[:, None] >= positions[None, :]
    run_sums = enter_sums
    run_counts = enter_counts
    outputs = []
    for block_id in range(blocks_here):
        offset = block_id * BLOCK
        survive = 1.0 - flags[block_id]
        cache_sums = survive * run_sums
        cache_counts = survive * run_counts
        code_means = (cache_sums / jnp.maximum(cache_counts, 1.0)[..., None]).astype(jnp.bfloat16)
        count_bias = jnp.where(cache_counts > 0, jnp.log(jnp.maximum(cache_counts, 1.0)), NEGATIVE)
        query_part = queries[0, offset : offset + BLOCK].reshape(BLOCK, HEADS, HEAD_DIM)
        value_part = values[0, offset : offset + BLOCK].reshape(BLOCK, HEADS, HEAD_DIM)
        code_scores = (
            jnp.einsum(
                "thd,hsd->hts", query_part, codebook_half, preferred_element_type=jnp.float32
            )
            * score_scale
            + count_bias[:, None, :]
        )
        key_codes = jnp.einsum(
            "hts,hsd->htd", hot_list[block_id], codebook_half, preferred_element_type=jnp.float32
        ).astype(jnp.bfloat16)
        local_scores = jnp.where(
            causal[None],
            jnp.einsum("ihd,hjd->hij", query_part, key_codes, preferred_element_type=jnp.float32)
            * score_scale,
            NEGATIVE,
        )
        row_top = jnp.maximum(jnp.max(code_scores, axis=-1), jnp.max(local_scores, axis=-1))
        code_weights = jnp.exp(code_scores - row_top[..., None])
        local_weights = jnp.where(causal[None], jnp.exp(local_scores - row_top[..., None]), 0.0)
        denominator = jnp.sum(code_weights, axis=-1) + jnp.sum(local_weights, axis=-1)
        mixed_part = jnp.einsum(
            "hts,hsd->htd",
            code_weights.astype(jnp.bfloat16),
            code_means,
            preferred_element_type=jnp.float32,
        )
        mixed_part = mixed_part + jnp.einsum(
            "hij,jhd->hid",
            local_weights.astype(jnp.bfloat16),
            value_part,
            preferred_element_type=jnp.float32,
        )
        out_rows = (
            (mixed_part / denominator[..., None])
            .transpose(1, 0, 2)
            .reshape(BLOCK, HEADS * HEAD_DIM)
            .astype(jnp.bfloat16)
        )
        outputs.append(out_rows)
        run_sums = cache_sums + value_sums[block_id]
        run_counts = cache_counts + value_counts[block_id]
    mixed = jnp.concatenate(outputs, axis=0)[None]
    return (mixed, codebook_out)


def solution(mesh):
    placed = (
        P("dp", "seq", None),
        P("dp", "seq", None),
        P("dp", "seq", None),
        P("dp", None, "seq"),
        P("dp", "seq"),
        P(),
        P(),
    )
    return jax.shard_map(
        shards,
        mesh=mesh,
        in_specs=placed,
        out_specs=(P("dp", "seq", None), P(None, "dp", None)),
        check_vma=False,
    )
```

profile of v0, /device:TPU:103, one launch (start us, length us, event | category | flops | bytes accessed | tf_op | source)
XLA Modules:
  0.0 883.3 jit_solution(4098301958992712305)
XLA Ops:
  75.9 63.2 %all-reduce = f32[32]{0:T(128)S(1)} all-reduce(f32[32]{0:T(128)S(1)} %bitcast_dynamic-update-slice_fusion), channel_id=1, replica_groups=mesh['dp'=4,'seq'=32] {'seq'}, use_global_device_ids=true, to_apply=%add | all-reduce | flops 32 | bytes 256
  139.1 67.3 %psum.15 = f32[16,512]{1,0:T(8,128)S(1)} all-reduce(f32[16,512]{1,0:T(8,128)S(1)} %get-tuple-element.93), channel_id=1, replica_groups=mesh['dp'=4,'seq'=32] {'dp','seq'}, use_global_device_ids=true, to_apply=%region_3.0 | all-reduce | flops 8192 | bytes 65536 | tf_op jit(solution)/shard_map/psum | solution.py:74
  206.6 285.1 %all-reduce.3.cloned.1.call-done = f32[16,512,128]{2,1,0:T(8,128)} async-done(((f32[16,512,128]{2,1,0:T(8,128)}), f32[16,512,128]{2,1,0:T(8,128)}) %all-reduce.3.cloned.1.call-update) | async-done | bytes 4194320 | tf_op jit(solution)/shard_map/psum | solution.py:74
  497.9 10.2 %fusion.14 = (f32[16,512]{1,0:T(8,128)S(1)}, f32[16,512,512]{2,1,0:T(8,128)}) fusion(pred[512,512]{0,1:T(8,128)(4,1)S(1)} %iota_compare_fusion.12, bf16[512,16,128]{0,2,1:T(8,128)(2,1)} %bitcast.107, bf16[16,512,128]{2,1,0:T(8,128)(2,1)S(1)} %get-tuple-element.82, s32[16,512]{1,0:T(8,128)S(1)} %get-tuple-element.95), kind=kOutput, calls=%fused_computation.27 | convolution fusion | flops 2165301248 | bytes 21299200 | tf_op jit(solution)/shard_map/ihd,hjd->hij/dot_general | solution.py:124
  510.6 261.9 %while.14 = (s32[]{:T(128)}, f32[16,512,128]{2,1,0:T(8,128)}, f32[16,512]{1,0:T(8,128)S(1)}, s32[]{:T(128)}, f32[32,16,512,128]{3,2,1,0:T(8,128)}, /*index=5*/f3...) while((s32[]{:T(128)}, f32[16,512,128]{2,1,0:T(8,128)}, ...), condition=%wide.region_5.6_spmd, body=%wide.region_4.5_spmd.sunk | while | flops 2113542 | bytes 12681379 | solution.py:27
  511.1 6.6 bitcast_add_fusion.4
  519.6 6.6 bitcast_add_fusion.4
  528.0 6.6 bitcast_add_fusion.4
  536.5 6.6 bitcast_add_fusion.4
  544.9 6.6 bitcast_add_fusion.4
  553.4 6.6 bitcast_add_fusion.4
  561.8 6.6 bitcast_add_fusion.4
  570.3 6.6 bitcast_add_fusion.4
  578.7 6.6 bitcast_add_fusion.4
  587.2 6.6 bitcast_add_fusion.4
  595.6 6.6 bitcast_add_fusion.4
  604.1 6.6 bitcast_add_fusion.4
  621.0 6.6 bitcast_add_fusion.4
  654.8 6.6 bitcast_add_fusion.4
  680.1 6.6 bitcast_add_fusion.4
  688.5 6.6 bitcast_add_fusion.4
  713.9 6.6 bitcast_add_fusion.4
  722.3 6.6 bitcast_add_fusion.4
  747.7 6.6 bitcast_add_fusion.4
  756.1 6.6 bitcast_add_fusion.4
  772.5 8.2 bitcast_reduce_fusion.1
  780.7 22.1 %fusion.20 = (f32[16,512]{1,0:T(8,128)S(1)}, f32[16,512]{1,0:T(8,128)S(1)}, f32[16,512]{1,0:T(8,128)S(1)}, f32[16,512,512]{2,1,0:T(8,128)}) fusion(f32[16,512,512]{2,1,0:T(8,128)} %get-tuple-element.107, f32[16,512]{1,0:T(8,128)S(1)} %max.29, pred[512,512]{0,1:T(8,128)(4,1)S(1)} %iota_compare_fusion.12, f32[16,512]{1,0:T(8,128)S(1)} %get-tuple-element.97, ...), kind=kOutput, calls=%fused_computation.33 | convolution fusion | flops 2203033600 | bytes 54984704 | tf_op jit(solution)/shard_map/ihd,hjd->hij/dot_general | solution.py:124
  802.8 9.5 %fusion.26 = f32[16,512,128]{1,2,0:T(8,128)S(1)} fusion(f32[16,512,512]{2,1,0:T(8,128)} %get-tuple-element.105, f32[16,512]{1,0:T(8,128)S(1)} %max.29, f32[16,512]{1,0:T(8,128)S(1)} %get-tuple-element.97, f32[16,512,128]{2,1,0:T(8,128)} %get-tuple-element.62, f32[16,512]{1,0:T(8,128)S(1)} %get-tuple-element.96, f32[]{:T(128)} %bitcast.8), kind=kOutput, calls=%fused_computation.38 | convolution fusion | flops 1093664768 | bytes 25264132 | tf_op jit(solution)/shard_map/hts,hsd->htd/dot_general | solution.py:132
  812.4 9.3 %fusion.47 = bf16[512,16,128]{0,2,1:T(8,128)(2,1)} fusion(f32[16,512,128]{1,2,0:T(8,128)S(1)} %fusion.26, f32[512,16]{0,1:T(8,128)S(1)} %add_bitcast_fusion.1, bf16[512,16,128]{0,2,1:T(8,128)(2,1)S(1)} %bitcast.112, f32[16,512,512]{2,1,0:T(8,128)} %get-tuple-element.107, f32[16,512]{1,0:T(8,128)S(1)} %max.29, pred[512,512]{0,1:T(8,128)(4,1)S(1)} %iota_compare_fusion.12), kind=kOutput, calls=%fused_computation.59 | convolution fusion | flops 1097859072 | bytes 25493504 | tf_op jit(solution)/shard_map/hij,jhd->hid/dot_general | solution.py:138
  830.0 16.9 %fusion.22 = (f32[16,512]{1,0:T(8,128)S(1)}, f32[16,512]{1,0:T(8,128)S(1)}) fusion(f32[16,512,512]{2,1,0:T(8,128)} %get-tuple-element.108, f32[16,512]{1,0:T(8,128)S(1)} %max.31, pred[512,512]{0,1:T(8,128)(4,1)S(1)} %iota_compare_fusion.12, f32[16,512]{1,0:T(8,128)S(1)} %get-tuple-element.91, f32[16,512,512]{2,1,0:T(8,128)S(1)} %get-tuple-element.103), kind=kLoop, calls=%fused_computation.35 | loop fusion | flops 37732352 | bytes 33947648 | tf_op jit(solution)/shard_map/reduce_sum | solution.py:131
  846.9 10.3 %fusion.24 = f32[16,512,128]{1,2,0:T(8,128)} fusion(f32[16,512,512]{2,1,0:T(8,128)} %copy-done.1, f32[16,512]{1,0:T(8,128)S(1)} %max.31, f32[16,512]{1,0:T(8,128)S(1)} %get-tuple-element.91, f32[16,512,128]{2,1,0:T(8,128)S(1)} %copy-done.11, f32[16,512,128]{2,1,0:T(8,128)S(1)} %copy-done, f32[16,512]{1,0:T(8,128)S(1)} %get-tuple-element.90, f32[]{:T(128)} %bitcast.8, ...), kind=kOutput, calls=%fused_computation.37 | convolution fusion | flops 1095761920 | bytes 29458440 | tf_op jit(solution)/shard_map/hts,hsd->htd/dot_general | solution.py:132
  857.2 10.3 %fusion.46 = bf16[512,16,128]{0,2,1:T(8,128)(2,1)} fusion(f32[16,512,128]{1,2,0:T(8,128)} %fusion.24, f32[512,16]{0,1:T(8,128)S(1)} %add_bitcast_fusion, bf16[512,16,128]{0,2,1:T(8,128)(2,1)S(1)} %bitcast.110, f32[16,512,512]{2,1,0:T(8,128)} %get-tuple-element.108, f32[16,512]{1,0:T(8,128)S(1)} %max.31, pred[512,512]{0,1:T(8,128)(4,1)S(1)} %iota_compare_fusion.12), kind=kOutput, calls=%fused_computation.57 | convolution fusion | flops 1097859072 | bytes 25493504 | tf_op jit(solution)/shard_map/hij,jhd->hid/dot_general | solution.py:138
  (141 shorter events, 221.3 us)
Async XLA Ops:
  8.0 483.7 %all-reduce.3.cloned.1.call-start = ((), (), s32[]{:S(2)}) async-start(), calls=%async_computation | async-start | bytes 8388608 | tf_op jit(solution)/shard_map/psum | solution.py:74
  19.2 5.8 copy-start.6
  30.7 0.7 copy-start.8
  30.8 477.4 %all-gather.7.cloned.1.call-start = ((), (), s32[]{:S(2)}) async-start(), calls=%async_computation.2 | async-start | bytes 1081344 | tf_op jit(solution)/shard_map/all_gather | solution.py:19
  38.6 469.6 %all-gather.5.cloned.1.call-start = ((), (), s32[]{:S(2)}) async-start(), calls=%async_computation.1 | async-start | bytes 138412032 | tf_op jit(solution)/shard_map/all_gather | solution.py:19
  49.1 7.7 copy-start.3
  54.9 1.9 copy-start.10
  68.1 6.5 copy-start.9
  68.1 138.4 %copy-start.7 = (f32[16,512]{1,0:T(8,128)S(1)}, f32[16,512]{1,0:T(8,128)}, u32[]{:S(2)}) copy-start(f32[16,512]{1,0:T(8,128)} %param.15) | copy-start | bytes 98308
  802.8 9.6 %copy-start.5 = (bf16[1,512,2048]{1,2,0:T(8,128)(2,1)S(1)}, bf16[1,512,2048]{1,2,0:T(8,128)(2,1)}, u32[]{:S(2)}) copy-start(bf16[1,512,2048]{1,2,0:T(8,128)(2,1)} %copy.88) | copy-start | bytes 6291460
  830.0 16.9 %copy-start.1 = (f32[16,512,512]{2,1,0:T(8,128)}, f32[16,512,512]{2,1,0:T(8,128)S(1)}, u32[]{:S(2)}) copy-start(f32[16,512,512]{2,1,0:T(8,128)S(1)} %get-tuple-element.103) | copy-start | bytes 50331652
  830.0 16.9 %copy-start = (f32[16,512,128]{2,1,0:T(8,128)S(1)}, f32[16,512,128]{2,1,0:T(8,128)}, u32[]{:S(2)}) copy-start(f32[16,512,128]{2,1,0:T(8,128)} %get-tuple-element.62) | copy-start | bytes 12582916
  830.0 16.9 %copy-start.11 = (f32[16,512,128]{2,1,0:T(8,128)S(1)}, f32[16,512,128]{2,1,0:T(8,128)}, u32[]{:S(2)}) copy-start(f32[16,512,128]{2,1,0:T(8,128)} %copy-done.10) | copy-start | bytes 12582916
  846.9 10.3 %copy-start.4 = (bf16[1,512,2048]{1,2,0:T(8,128)(2,1)S(1)}, bf16[1,512,2048]{1,2,0:T(8,128)(2,1)}, u32[]{:S(2)}) copy-start(bf16[1,512,2048]{1,2,0:T(8,128)(2,1)} %copy.89) | copy-start | bytes 6291460
  867.6 4.1 copy-start.2
Sparse Core Ops, SparseCore 0:
  30.9 460.7 all-reduce.2
Sparse Core Ops, SparseCore 1:
  38.7 42.5 all-gather.6
  83.9 378.2 all-gather.4
where the time goes:
time: 887 us; the launch traced here: 883 us
  other arithmetic  293 us (33%)
  waiting for transfers between devices  285 us (32%)
  blocking collectives  131 us (15%)
  matrix products  107 us (12%)
  local copies, waits for them, and re-layouts  48.4 us (5%)
  between operations  18.3 us (2%)
    psum x1, waiting for transfers between devices, shards(): total_keys, total_counts = lax.psum((key_sums, code_counts), ('dp', 'seq'))  285 us
    add x31, other arithmetic, join_segments(): later[0] + survive * earlier[0]  203 us
    psum x1, blocking collectives, shards(): total_keys, total_counts = lax.psum((key_sums, code_counts), ('dp', 'seq'))  67.3 us
    unnamed x1, blocking collectives  63.2 us
    add x31, other arithmetic, join_segments(): later[1] + survive * earlier[1]  41.4 us
    dot_general x2, matrix products, shards(): jnp.einsum('ihd,hjd->hij', query_part, key_codes, preferred_element_type=...  32.3 us
    unnamed x33, local copies, waits for them, and re-layouts  23.2 us
    dot_general x2, matrix products, shards(): jnp.einsum('hts,hsd->htd', code_weights.astype(jnp.bfloat16), code_means,...  19.9 us
  transfers between devices with their start and end apart: 3, of which 1 were waited for; matrix products, arithmetic and copies ran while one was open for 6% of the time, Pallas kernels for 0%

commit v1 on v0

v1 whole, which is shorter than its diff:
```python
import functools

import jax
import jax.numpy as jnp
from jax import lax
from jax.experimental import pallas as pl
from jax.experimental.pallas import tpu as pltpu
from jax.sharding import PartitionSpec as P

HEADS = 16
HEAD_DIM = 128
CODES = 512
BLOCK = 512
TOK_DEV = 1024
RETAIN = 0.9
NEGATIVE = -1e30
SCORE_TO_LOG2 = 1.4426950408889634 * HEAD_DIM**-0.5

KEY_ROWS = 1032
VAL_ROWS = 264
CHIPS = 16
DPS = 4
F32 = jnp.float32
BF16 = jnp.bfloat16
MESH = pl.DeviceIdType.MESH


def column(row):
    return jnp.broadcast_to(row, (128, 128)).T


def head_row(ref, h, lanes, batched):
    tile = pl.ds(pl.multiple_of((h // 8) * 8, 8), 8)
    rows = ref[0, tile, lanes] if batched else ref[tile, lanes]
    picked = lax.broadcasted_iota(jnp.int32, rows.shape, 0) == h % 8
    return jnp.sum(jnp.where(picked, rows, jnp.zeros_like(rows)), axis=0, keepdims=True)


def stats_kernel(starts_ref, codes_ref, k_ref, v_ref, kin_ref, tail_ref, head_ref, first_ref):
    h = pl.program_id(0)
    f0 = starts_ref[0, 0].astype(F32)
    f1 = starts_ref[0, 1].astype(F32)
    s1 = 1.0 - f1
    code_iota = lax.broadcasted_iota(jnp.int32, (CODES, BLOCK), 0)
    lane = lax.broadcasted_iota(jnp.int32, (BLOCK, 128), 1).astype(F32)
    place = lax.broadcasted_iota(jnp.int32, (BLOCK, 128), 0).astype(F32)
    sums, counts = [], []
    for b in range(2):
        rows = slice(b * BLOCK, (b + 1) * BLOCK)
        code_row = head_row(codes_ref, h, rows, True)
        hot = jnp.where(code_iota == code_row, 1.0, 0.0).astype(BF16)
        pair = jnp.concatenate([k_ref[0, rows, :], v_ref[0, rows, :]], axis=1)
        sums.append(jnp.dot(hot, pair, preferred_element_type=F32))
        code_col = jnp.broadcast_to(code_row.astype(F32), (128, BLOCK)).T
        counted = []
        for r in range(4):
            same = code_col == lane + 128.0 * r
            counted.append(jnp.sum(jnp.where(same, 1.0, 0.0), axis=0, keepdims=True))
            first_ref[0, b : b + 1, r * 128 : (r + 1) * 128] = jnp.min(
                jnp.where(same, place, float(BLOCK)), axis=0, keepdims=True
            )
        counts.append(counted)
    first_ref[0, 2:8, :] = jnp.zeros((6, CODES), F32)
    key_sums = sums[0][:, :128] + sums[1][:, :128]
    key_counts = jnp.concatenate([counts[0][r] + counts[1][r] for r in range(4)], axis=0)

    @pl.when(h % 2 == 0)
    def _():
        kin_ref[0, 0:512, :] = key_sums
        kin_ref[0, 1024:1028, :] = key_counts

    @pl.when(h % 2 == 1)
    def _():
        kin_ref[0, 512:1024, :] = key_sums
        kin_ref[0, 1028:1032, :] = key_counts

    flag = jnp.broadcast_to(jnp.maximum(f0, f1), (1, 128))
    pad = jnp.zeros((5, 128), F32)
    for g in range(2):
        part = slice(g * 256, (g + 1) * 256)
        head_ref[g, 0:256, :] = sums[0][part, 128:]
        tail_ref[g, 0:256, :] = s1 * sums[0][part, 128:] + sums[1][part, 128:]
        early = [counts[0][2 * g], counts[0][2 * g + 1]]
        late = [s1 * counts[0][2 * g + i] + counts[1][2 * g + i] for i in range(2)]
        head_ref[g, 256:264, :] = jnp.concatenate(early + [flag, pad], axis=0)
        tail_ref[g, 256:264, :] = jnp.concatenate(late + [flag, pad], axis=0)


def statistics(starts, codes, keys, values):
    token = pl.BlockSpec((1, TOK_DEV, HEAD_DIM), lambda h: (0, 0, h))
    packed = pl.BlockSpec((2, VAL_ROWS, 128), lambda h: (h, 0, 0))
    return pl.pallas_call(
        stats_kernel,
        name="statistics",
        grid=(HEADS,),
        out_shape=(
            jax.ShapeDtypeStruct((8, KEY_ROWS, 128), F32),
            jax.ShapeDtypeStruct((32, VAL_ROWS, 128), F32),
            jax.ShapeDtypeStruct((32, VAL_ROWS, 128), F32),
            jax.ShapeDtypeStruct((HEADS, 8, CODES), F32),
        ),
        in_specs=[
            pl.BlockSpec(memory_space=pltpu.SMEM),
            pl.BlockSpec((1, HEADS, TOK_DEV), lambda h: (0, 0, 0)),
            token,
            token,
        ],
        out_specs=[
            pl.BlockSpec((1, KEY_ROWS, 128), lambda h: (h // 2, 0, 0)),
            packed,
            packed,
            pl.BlockSpec((1, 8, CODES), lambda h: (h, 0, 0)),
        ],
        compiler_params=pltpu.CompilerParams(vmem_limit_bytes=40 << 20),
    )(starts, codes, keys, values)


def exchange_kernel(
    kin, vin, kout, vout,
    k0, kchip, k1, s1, k2, own, v0, chip, v1, ent, v2, back,
    core_send, core_recv, dp_send, dp_recv, chip_send, chip_recv,
):
    y = lax.axis_index("dp")
    me = lax.axis_index("seq")
    c = me % 2
    p = me // 2
    other = {"seq": p * 2 + (1 - c)}

    def at_chip(j):
        return {"seq": j * 2 + c}

    def remote(src, dst, send, recv, device):
        return pltpu.make_async_remote_copy(
            src_ref=src, dst_ref=dst, send_sem=send, recv_sem=recv,
            device_id=device, device_id_type=MESH,
        )

    def others(count, mine, body):
        def step(k, carry):
            body(lax.rem(mine + k, count))
            return carry

        lax.fori_loop(1, count, step, 0)

    barrier = pltpu.get_barrier_semaphore()

    def greet(device):
        pl.semaphore_signal(barrier, inc=1, device_id=device, device_id_type=MESH)

    greet(other)
    others(CHIPS, p, lambda j: greet(at_chip(j)))
    others(DPS, y, lambda j: greet({"dp": j}))
    pl.semaphore_wait(barrier, 1 + (CHIPS - 1) + (DPS - 1))

    key_core = remote(kin.at[pl.ds(4 * (1 - c), 4)], k0, core_send.at[0], core_recv.at[0], other)
    val_core = remote(vin.at[pl.ds(16 * (1 - c), 16)], v0, core_send.at[1], core_recv.at[1], other)
    key_core.start()
    val_core.start()

    key_core.wait_recv()

    def add_core(q, carry):
        kchip[q] = kin[4 * c + q] + k0[q]
        return carry

    lax.fori_loop(0, 4, add_core, 0)

    def key_dp(j, slot, sem):
        return remote(kchip.at[j], k1.at[slot], dp_send.at[0, j], dp_recv.at[0, sem], {"dp": j})

    others(DPS, y, lambda j: key_dp(j, y, y).start())

    val_core.wait_recv()

    def join_cores(g, carry):
        mine = vin[16 * c + g]
        theirs = v0[g]
        early = jnp.where(c == 0, mine, theirs)
        late = jnp.where(c == 0, theirs, mine)
        chip[g] = late + (1.0 - late[258:259, :]) * early
        return carry

    lax.fori_loop(0, 16, join_cores, 0)

    def val_out(j, slot, sem):
        return remote(
            chip.at[j], v1.at[slot], chip_send.at[0, j], chip_recv.at[0, sem], at_chip(j)
        )

    others(CHIPS, p, lambda j: val_out(j, p, p).start())
    v1[p] = chip[p]

    k1[y] = kchip[y]
    others(DPS, y, lambda j: key_dp(j, j, j).wait_recv())
    tallied = (k1[0, 1024:1032, :] + k1[1, 1024:1032, :]) + (k1[2, 1024:1032, :] + k1[3, 1024:1032, :])

    def add_dp(j, carry):
        rows = pl.ds(pl.multiple_of(j * 64, 64), 64)
        s1[j, 0:64, :] = (k1[0, rows, :] + k1[1, rows, :]) + (k1[2, rows, :] + k1[3, rows, :])
        s1[j, 64:72, :] = tallied
        return carry

    lax.fori_loop(0, CHIPS, add_dp, 0)

    def key_out(j, slot, sem):
        return remote(s1.at[j], k2.at[slot], chip_send.at[1, j], chip_recv.at[1, sem], at_chip(j))

    others(CHIPS, p, lambda j: key_out(j, p, p).start())
    k2[p] = s1[p]

    others(CHIPS, p, lambda j: val_out(j, j, j).wait_recv())

    def scan(j, run):
        ent[j] = run
        part = v1[j]
        return part + (1.0 - part[258:259, :]) * run

    lax.fori_loop(0, CHIPS, scan, jnp.zeros((VAL_ROWS, 128), F32))

    others(CHIPS, p, lambda j: key_out(j, j, j).wait_recv())
    total = lax.fori_loop(0, CHIPS, lambda j, run: run + k2[j], jnp.zeros((72, 128), F32))
    own[...] = total[0:64]
    quarter = 4 * c + y
    mine = pl.ds(pl.multiple_of(p * 64, 64), 64)
    kout[quarter, mine, :] = total[0:64]
    kout[quarter, 1024:1032, :] = total[64:72]

    def key_back(j, slot, sem):
        rows = pl.ds(pl.multiple_of(slot * 64, 64), 64)
        return remote(
            own, kout.at[quarter, rows], chip_send.at[2, j], chip_recv.at[2, sem], at_chip(j)
        )

    others(CHIPS, p, lambda j: key_back(j, p, p).start())

    def val_back(j, slot, sem):
        return remote(
            ent.at[j], v2.at[slot], chip_send.at[3, j], chip_recv.at[3, sem], at_chip(j)
        )

    others(CHIPS, p, lambda j: val_back(j, p, p).start())
    v2[p] = ent[p]

    others(CHIPS, p, lambda j: key_back(j, j, j).wait_recv())

    def key_spread(j, held, sem):
        part = kout.at[4 * c + held]
        return remote(part, part, dp_send.at[1, j], dp_recv.at[1, sem], {"dp": j})

    def key_share(held, half):
        part = kout.at[4 * half + held]
        return remote(part, part, core_send.at[3 + held], core_recv.at[3 + held], other)

    others(DPS, y, lambda j: key_spread(j, y, y).start())
    key_share(y, c).start()

    def pass_on(j):
        key_spread(j, j, j).wait_recv()
        key_share(j, c).start()

    others(DPS, y, pass_on)

    others(CHIPS, p, lambda j: val_back(j, j, j).wait_recv())

    def split_cores(g, carry):
        early = jnp.where(c == 0, vin[16 * c + g], v0[g])
        first = v2[g]
        second = early + (1.0 - early[258:259, :]) * first
        vout[16 * c + g] = jnp.where(c == 0, first, second)
        back[g] = jnp.where(c == 0, second, first)
        return carry

    lax.fori_loop(0, 16, split_cores, 0)
    half = vout.at[pl.ds(16 * c, 16)]
    val_core_back = remote(back, half, core_send.at[2], core_recv.at[2], other)
    val_core_back.start()

    def finish(held, carry):
        key_share(held, 1 - c).wait_recv()
        return carry

    lax.fori_loop(0, DPS, finish, 0)
    remote(
        back, vout.at[pl.ds(16 * (1 - c), 16)], core_send.at[2], core_recv.at[2], other
    ).wait_recv()

    key_core.wait_send()
    val_core.wait_send()
    val_core_back.wait_send()

    def sent_dp(j):
        key_dp(j, j, j).wait_send()
        key_spread(j, y, j).wait_send()

    others(DPS, y, sent_dp)

    def sent_core(held, carry):
        key_share(held, c).wait_send()
        return carry

    lax.fori_loop(0, DPS, sent_core, 0)

    def sent_chip(j):
        val_out(j, j, j).wait_send()
        key_out(j, j, j).wait_send()
        key_back(j, j, j).wait_send()
        val_back(j, j, j).wait_send()

    others(CHIPS, p, sent_chip)


def exchange(kin, vin):
    whole = pl.BlockSpec(memory_space=pltpu.VMEM)
    return pl.pallas_call(
        exchange_kernel,
        name="exchange",
        out_shape=(
            jax.ShapeDtypeStruct((8, KEY_ROWS, 128), F32),
            jax.ShapeDtypeStruct((32, VAL_ROWS, 128), F32),
        ),
        in_specs=[whole, whole],
        out_specs=[whole, whole],
        scratch_shapes=[
            pltpu.VMEM((4, KEY_ROWS, 128), F32),
            pltpu.VMEM((4, KEY_ROWS, 128), F32),
            pltpu.VMEM((4, KEY_ROWS, 128), F32),
            pltpu.VMEM((CHIPS, 72, 128), F32),
            pltpu.VMEM((CHIPS, 72, 128), F32),
            pltpu.VMEM((64, 128), F32),
            pltpu.VMEM((16, VAL_ROWS, 128), F32),
            pltpu.VMEM((16, VAL_ROWS, 128), F32),
            pltpu.VMEM((CHIPS, VAL_ROWS, 128), F32),
            pltpu.VMEM((CHIPS, VAL_ROWS, 128), F32),
            pltpu.VMEM((CHIPS, VAL_ROWS, 128), F32),
            pltpu.VMEM((16, VAL_ROWS, 128), F32),
            pltpu.SemaphoreType.DMA((7,)),
            pltpu.SemaphoreType.DMA((7,)),
            pltpu.SemaphoreType.DMA((2, DPS)),
            pltpu.SemaphoreType.DMA((2, DPS)),
            pltpu.SemaphoreType.DMA((4, CHIPS)),
            pltpu.SemaphoreType.DMA((4, CHIPS)),
        ],
        compiler_params=pltpu.CompilerParams(
            collective_id=0, has_side_effects=True, vmem_limit_bytes=56 << 20
        ),
    )(kin, vin)


def attend_kernel(
    starts_ref, codes_ref, q_ref, v_ref, keys_ref, enter_ref, head_ref, first_ref,
    cent_ref, old_ref, out_ref, book_out_ref, book_ref,
):
    h = pl.program_id(0)
    odd = h % 2
    alive = [1.0 - starts_ref[0, b].astype(F32) for b in range(2)]

    tallied = keys_ref[0, 1024:1032, :]
    tallied = jnp.where(odd == 0, tallied[0:4], tallied[4:8])
    for r in range(4):
        rows = slice(r * 128, (r + 1) * 128)
        old = column(head_row(old_ref, h, rows, False))
        now = column(tallied[r : r + 1])
        sums = keys_ref[0, pl.ds(pl.multiple_of(odd * 512 + r * 128, 128), 128), :]
        book_ref[rows, :] = (RETAIN * old * cent_ref[0, rows, :] + (1.0 - RETAIN) * sums) / (
            RETAIN * old + (1.0 - RETAIN) * now
        )
    share = pl.multiple_of(lax.axis_index("dp") * 128, 128)
    book_out_ref[0] = book_ref[pl.ds(share, 128), :]
    book = book_ref[...].astype(BF16)

    def unpacked(ref):
        sums = jnp.concatenate([ref[0, 0:256, :], ref[1, 0:256, :]], axis=0)
        counts = jnp.concatenate(
            [ref[0, 256:257, :], ref[0, 257:258, :], ref[1, 256:257, :], ref[1, 257:258, :]],
            axis=1,
        )
        return sums, counts

    sums, counts = unpacked(enter_ref)
    code_iota = lax.broadcasted_iota(jnp.int32, (CODES, BLOCK), 0)
    square_row = lax.broadcasted_iota(jnp.int32, (128, 128), 0)
    ones_column = jnp.where(
        lax.broadcasted_iota(jnp.int32, (BLOCK, 128), 1) == 0, 1.0, 0.0
    ).astype(BF16)
    half = BLOCK // 2
    causal = lax.broadcasted_iota(jnp.int32, (half, half), 0) >= lax.broadcasted_iota(
        jnp.int32, (half, half), 1
    )
    place = lax.broadcasted_iota(jnp.int32, (half, CODES), 0).astype(F32)
    for b in range(2):
        if b == 1:
            more, added = unpacked(head_ref)
            sums, counts = sums + more, counts + added
        sums, counts = alive[b] * sums, alive[b] * counts
        present = counts > 0
        bias = jnp.where(present, jnp.log2(jnp.maximum(counts, 1.0)), 0.0)
        opens = jnp.where(present, -1.0, first_ref[0, b : b + 1, :])
        high = jnp.floor(counts * (1.0 / 256.0)) * 256.0
        low = counts - high
        columns = []
        for r in range(4):
            lanes = slice(r * 128, (r + 1) * 128)
            columns.append(
                jnp.where(
                    square_row == 0, high[:, lanes], jnp.where(square_row == 1, low[:, lanes], 0.0)
                ).T
            )
        cache = jnp.concatenate([sums, jnp.concatenate(columns, axis=0)], axis=1).astype(BF16)
        rows = slice(b * BLOCK, (b + 1) * BLOCK)
        code_row = head_row(codes_ref, h, rows, True)
        hot = jnp.where(code_iota == code_row, 1.0, 0.0).astype(BF16)
        local = jnp.concatenate([v_ref[0, rows, :], ones_column], axis=1)
        for i in range(2):
            at = slice(b * BLOCK + i * half, b * BLOCK + (i + 1) * half)
            scores = lax.dot_general(
                q_ref[0, at, :], book, (((1,), (1,)), ((), ())), preferred_element_type=F32
            )
            scores = scores * SCORE_TO_LOG2
            top = jnp.max(
                jnp.where(opens <= place + float(i * half), scores + bias, NEGATIVE),
                axis=1,
                keepdims=True,
            )
            weight = jnp.exp2(jnp.minimum(scores - top, 0.0)).astype(BF16)
            acc = jnp.dot(weight, cache, preferred_element_type=F32)
            if i == 1:
                early = jnp.dot(weight, hot[:, :half], preferred_element_type=F32).astype(BF16)
                acc = acc + jnp.dot(early, local[:half], preferred_element_type=F32)
            near = jnp.dot(weight, hot[:, i * half : (i + 1) * half], preferred_element_type=F32)
            near = jnp.where(causal, near, 0.0).astype(BF16)
            acc = acc + jnp.dot(
                near, local[i * half : (i + 1) * half], preferred_element_type=F32
            )
            out_ref[0, at, :] = (acc[:, :128] / (acc[:, 128:129] + acc[:, 129:130])).astype(BF16)


def attend(starts, codes, queries, values, keys, enter, head, first, centroids, old):
    token = pl.BlockSpec((1, TOK_DEV, HEAD_DIM), lambda h: (0, 0, h))
    packed = pl.BlockSpec((2, VAL_ROWS, 128), lambda h: (h, 0, 0))
    return pl.pallas_call(
        attend_kernel,
        name="attend",
        grid=(HEADS,),
        out_shape=(
            jax.ShapeDtypeStruct((1, TOK_DEV, HEADS * HEAD_DIM), BF16),
            jax.ShapeDtypeStruct((HEADS, CODES // DPS, HEAD_DIM), F32),
        ),
        in_specs=[
            pl.BlockSpec(memory_space=pltpu.SMEM),
            pl.BlockSpec((1, HEADS, TOK_DEV), lambda h: (0, 0, 0)),
            token,
            token,
            pl.BlockSpec((1, KEY_ROWS, 128), lambda h: (h // 2, 0, 0)),
            packed,
            packed,
            pl.BlockSpec((1, 8, CODES), lambda h: (h, 0, 0)),
            pl.BlockSpec((1, CODES, HEAD_DIM), lambda h: (h, 0, 0)),
            pl.BlockSpec((HEADS, CODES), lambda h: (0, 0)),
        ],
        out_specs=[token, pl.BlockSpec((1, CODES // DPS, HEAD_DIM), lambda h: (h, 0, 0))],
        scratch_shapes=[pltpu.VMEM((CODES, HEAD_DIM), F32)],
        compiler_params=pltpu.CompilerParams(vmem_limit_bytes=40 << 20),
    )(starts, codes, queries, values, keys, enter, head, first, centroids, old)


def shards(queries, keys, values, codes, starts, old_centroids, old_counts):
    kin, tail, head, first = statistics(starts, codes, keys, values)
    total, enter = exchange(kin, tail)
    return attend(
        starts, codes, queries, values, total, enter, head, first, old_centroids, old_counts
    )


def solution(mesh):
    placed = (
        P("dp", "seq", None),
        P("dp", "seq", None),
        P("dp", "seq", None),
        P("dp", None, "seq"),
        P("dp", "seq"),
        P(),
        P(),
    )
    return jax.shard_map(
        shards,
        mesh=mesh,
        in_specs=placed,
        out_specs=(P("dp", "seq", None), P(None, "dp", None)),
        check_vma=False,
    )
```

time: 887 us -> 187 us (0.21)
  the two profiles are of different devices: /device:TPU:103 before, /device:TPU:0 now
where the time goes in v1:
time: 187 us; the launch traced here: 185 us
  Pallas kernels  172 us (92%)
  local copies, waits for them, and re-layouts  12.2 us (7%)
    pallas_call x1, Pallas kernels, exchange(): pl.pallas_call(exchange_kernel, name='exchange', out_shape=(jax.ShapeDtyp...  105 us
    pallas_call x1, Pallas kernels, attend(): pl.pallas_call(attend_kernel, name='attend', grid=(HEADS,), out_shape=(ja...  50 us
    pallas_call x1, Pallas kernels, statistics(): pl.pallas_call(stats_kernel, name='statistics', grid=(HEADS,), out_shape=...  16.9 us
    unnamed x22, local copies, waits for them, and re-layouts  12.2 us

profile of v1, /device:TPU:0, one launch (start us, length us, event | category | flops | bytes accessed | tf_op | source)
XLA Modules:
  0.0 185.0 jit_solution(304131785144705156)
XLA Ops:
  0.6 0.0 copy-start
  0.6 2.2 %copy-done = bf16[1,1024,2048]{2,1,0:T(8,128)(2,1)S(1)} copy-done((bf16[1,1024,2048]{2,1,0:T(8,128)(2,1)S(1)}, bf16[1,1024,2048]{2,1,0:T(8,128)(2,1)}, u32[]{:S(2)}) %copy-start) | copy-done | bytes 4194328
  2.8 0.0 copy-start.3
  2.8 2.2 %copy-done.3 = bf16[1,1024,2048]{2,1,0:T(8,128)(2,1)S(1)} copy-done((bf16[1,1024,2048]{2,1,0:T(8,128)(2,1)S(1)}, bf16[1,1024,2048]{2,1,0:T(8,128)(2,1)}, u32[]{:S(2)}) %copy-start.3) | copy-done | bytes 4194328
  5.0 0.0 copy-start.6
  5.0 0.8 copy-done.6
  5.8 0.0 copy-start.9
  5.9 0.7 copy-done.9
  6.5 16.9 %statistics.1 = (f32[8,1032,128]{2,1,0:T(8,128)S(1)}, f32[32,264,128]{2,1,0:T(8,128)}, f32[32,264,128]{2,1,0:T(8,128)}, f32[16,8,512]{2,1,0:T(8,128)S(1)}) custom-call(s32[1,2]{1,0:T(1,128)S(1)} %copy-done.9, s32[1,16,1024]{2,1,0:T(8,128)S(1)} %copy-done.6, bf16[1,1024,2048]{2,1,0:T(8,128)(2,1)S(1)} %copy-done.3, bf16[1,1024,2048]{2,1,0:T(8,128)(2,1)S(1)} %copy-done), custom_call_target="tpu_custom_call" | custom-call | tf_op jit(solution)/shard_map/statistics/pallas_call | solution.py:92
  23.4 0.0 copy-start.2
  23.4 2.0 %copy-done.2 = f32[8,1032,128]{2,1,0:T(8,128)} copy-done((f32[8,1032,128]{2,1,0:T(8,128)}, f32[8,1032,128]{2,1,0:T(8,128)S(1)}, u32[]{:S(2)}) %copy-start.2) | copy-done | bytes 4227096
  25.4 0.0 copy-start.1
  25.4 0.0 copy-start.7
  25.4 0.0 copy-start.8
  25.4 0.0 copy-start.10
  25.4 105.2 %exchange.1 = (f32[8,1032,128]{2,1,0:T(8,128)}, f32[32,264,128]{2,1,0:T(8,128)}) custom-call(f32[8,1032,128]{2,1,0:T(8,128)} %copy-done.2, f32[32,264,128]{2,1,0:T(8,128)} %get-tuple-element.9.vin), custom_call_target="tpu_custom_call" | custom-call | tf_op jit(solution)/shard_map/exchange/pallas_call | solution.py:314
  130.6 0.0 copy-done.1
  130.7 0.0 copy-done.7
  130.7 0.0 copy-done.8
  130.7 0.0 copy-done.10
  130.7 0.0 copy-start.4
  130.7 2.2 %copy-done.4 = bf16[1,1024,2048]{2,1,0:T(8,128)(2,1)S(1)} copy-done((bf16[1,1024,2048]{2,1,0:T(8,128)(2,1)S(1)}, bf16[1,1024,2048]{2,1,0:T(8,128)(2,1)}, u32[]{:S(2)}) %copy-start.4) | copy-done | bytes 4194328
  132.9 0.0 copy-start.5
  132.9 2.2 %copy-done.5 = f32[16,512,128]{2,1,0:T(8,128)S(1)} copy-done((f32[16,512,128]{2,1,0:T(8,128)S(1)}, f32[16,512,128]{2,1,0:T(8,128)}, u32[]{:S(2)}) %copy-start.5) | copy-done | bytes 4194328
  135.1 50.0 %attend.1 = (bf16[1,1024,2048]{2,1,0:T(8,128)(2,1)}, f32[16,128,128]{2,1,0:T(8,128)}) custom-call(s32[1,2]{1,0:T(1,128)S(1)} %copy-done.10, s32[1,16,1024]{2,1,0:T(8,128)S(1)} %copy-done.7, bf16[1,1024,2048]{2,1,0:T(8,128)(2,1)S(1)} %copy-done.4, bf16[1,1024,2048]{2,1,0:T(8,128)(2,1)S(1)} %copy-done.1, f32[8,1032,128]{2,1,0:T(8,128)} %get-tuple-element.10.keys_ref, ...), custom_call_target="tpu_custom_call" | custom-call | tf_op jit(solution)/shard_map/attend/pallas_call | solution.py:440
Async XLA Ops:
  0.6 2.2 %copy-start = (bf16[1,1024,2048]{2,1,0:T(8,128)(2,1)S(1)}, bf16[1,1024,2048]{2,1,0:T(8,128)(2,1)}, u32[]{:S(2)}) copy-start(bf16[1,1024,2048]{2,1,0:T(8,128)(2,1)} %v_ref.3) | copy-start | bytes 12582916
  2.8 2.2 %copy-start.3 = (bf16[1,1024,2048]{2,1,0:T(8,128)(2,1)S(1)}, bf16[1,1024,2048]{2,1,0:T(8,128)(2,1)}, u32[]{:S(2)}) copy-start(bf16[1,1024,2048]{2,1,0:T(8,128)(2,1)} %k_ref.1) | copy-start | bytes 12582916
  5.0 0.8 copy-start.6
  5.8 0.7 copy-start.9
  23.4 2.0 %copy-start.2 = (f32[8,1032,128]{2,1,0:T(8,128)}, f32[8,1032,128]{2,1,0:T(8,128)S(1)}, u32[]{:S(2)}) copy-start(f32[8,1032,128]{2,1,0:T(8,128)S(1)} %get-tuple-element.8.kin) | copy-start | bytes 12681220
  25.4 105.3 %copy-start.1 = (bf16[1,1024,2048]{2,1,0:T(8,128)(2,1)S(1)}, bf16[1,1024,2048]{2,1,0:T(8,128)(2,1)}, u32[]{:S(2)}) copy-start(bf16[1,1024,2048]{2,1,0:T(8,128)(2,1)} %v_ref.3) | copy-start | bytes 12582916
  25.4 105.3 %copy-start.7 = (s32[1,16,1024]{2,1,0:T(8,128)S(1)}, s32[1,16,1024]{2,1,0:T(8,128)}, u32[]{:S(2)}) copy-start(s32[1,16,1024]{2,1,0:T(8,128)} %codes_ref.3) | copy-start | bytes 196612
  25.4 105.3 %copy-start.8 = (f32[16,512]{1,0:T(8,128)S(1)}, f32[16,512]{1,0:T(8,128)}, u32[]{:S(2)}) copy-start(f32[16,512]{1,0:T(8,128)} %old_ref.1) | copy-start | bytes 98308
  25.4 105.3 %copy-start.10 = (s32[1,2]{1,0:T(1,128)S(1)}, s32[1,2]{1,0:T(1,128)}, u32[]{:S(2)}) copy-start(s32[1,2]{1,0:T(1,128)} %starts_ref.3) | copy-start | bytes 28
  130.7 2.2 %copy-start.4 = (bf16[1,1024,2048]{2,1,0:T(8,128)(2,1)S(1)}, bf16[1,1024,2048]{2,1,0:T(8,128)(2,1)}, u32[]{:S(2)}) copy-start(bf16[1,1024,2048]{2,1,0:T(8,128)(2,1)} %q_ref.1) | copy-start | bytes 12582916
  132.9 2.2 %copy-start.5 = (f32[16,512,128]{2,1,0:T(8,128)S(1)}, f32[16,512,128]{2,1,0:T(8,128)}, u32[]{:S(2)}) copy-start(f32[16,512,128]{2,1,0:T(8,128)} %cent_ref.1) | copy-start | bytes 12582916

commit v2 on v1

--- a/solution.py
+++ b/solution.py
@@ -111,7 +111,7 @@
             packed,
             pl.BlockSpec((1, 8, CODES), lambda h: (h, 0, 0)),
         ],
-        compiler_params=pltpu.CompilerParams(vmem_limit_bytes=40 << 20),
+        compiler_params=pltpu.CompilerParams(vmem_limit_bytes=60 << 20),
     )(starts, codes, keys, values)
 
 
@@ -383,10 +383,13 @@
         lax.broadcasted_iota(jnp.int32, (BLOCK, 128), 1) == 0, 1.0, 0.0
     ).astype(BF16)
     half = BLOCK // 2
-    causal = lax.broadcasted_iota(jnp.int32, (half, half), 0) >= lax.broadcasted_iota(
-        jnp.int32, (half, half), 1
+    causal = lax.broadcasted_iota(jnp.int32, (BLOCK, half), 0) >= lax.broadcasted_iota(
+        jnp.int32, (BLOCK, half), 1
     )
-    place = lax.broadcasted_iota(jnp.int32, (half, CODES), 0).astype(F32)
+    place = lax.broadcasted_iota(jnp.int32, (BLOCK, CODES), 0).astype(F32)
+    scores_all = lax.dot_general(
+        q_ref[0], book, (((1,), (1,)), ((), ())), preferred_element_type=F32
+    )
     for b in range(2):
         if b == 1:
             more, added = unpacked(head_ref)
@@ -410,28 +413,25 @@
         code_row = head_row(codes_ref, h, rows, True)
         hot = jnp.where(code_iota == code_row, 1.0, 0.0).astype(BF16)
         local = jnp.concatenate([v_ref[0, rows, :], ones_column], axis=1)
-        for i in range(2):
-            at = slice(b * BLOCK + i * half, b * BLOCK + (i + 1) * half)
-            scores = lax.dot_general(
-                q_ref[0, at, :], book, (((1,), (1,)), ((), ())), preferred_element_type=F32
-            )
-            scores = scores * SCORE_TO_LOG2
-            top = jnp.max(
-                jnp.where(opens <= place + float(i * half), scores + bias, NEGATIVE),
-                axis=1,
-                keepdims=True,
-            )
-            weight = jnp.exp2(jnp.minimum(scores - top, 0.0)).astype(BF16)
-            acc = jnp.dot(weight, cache, preferred_element_type=F32)
-            if i == 1:
-                early = jnp.dot(weight, hot[:, :half], preferred_element_type=F32).astype(BF16)
-                acc = acc + jnp.dot(early, local[:half], preferred_element_type=F32)
-            near = jnp.dot(weight, hot[:, i * half : (i + 1) * half], preferred_element_type=F32)
-            near = jnp.where(causal, near, 0.0).astype(BF16)
-            acc = acc + jnp.dot(
-                near, local[i * half : (i + 1) * half], preferred_element_type=F32
-            )
-            out_ref[0, at, :] = (acc[:, :128] / (acc[:, 128:129] + acc[:, 129:130])).astype(BF16)
+        scores = scores_all[b * BLOCK : (b + 1) * BLOCK] * SCORE_TO_LOG2
+        top = jnp.max(
+            jnp.where(opens <= place, scores + bias, NEGATIVE), axis=1, keepdims=True
+        )
+        weight = jnp.exp2(jnp.minimum(scores - top, 0.0)).astype(BF16)
+        near = jnp.dot(weight, hot[:, :half], preferred_element_type=F32)
+        near = jnp.where(causal, near, 0.0).astype(BF16)
+        far = jnp.dot(weight[half:], hot[:, half:], preferred_element_type=F32)
+        far = jnp.where(causal[:half], far, 0.0).astype(BF16)
+        acc = jnp.dot(weight, cache, preferred_element_type=F32)
+        acc = acc + jnp.dot(near, local[:half], preferred_element_type=F32)
+        acc_far = acc[half:] + jnp.dot(far, local[half:], preferred_element_type=F32)
+        top_rows = slice(b * BLOCK, b * BLOCK + half)
+        low_rows = slice(b * BLOCK + half, (b + 1) * BLOCK)
+        acc = acc[:half]
+        out_ref[0, top_rows, :] = (acc[:, :128] / (acc[:, 128:129] + acc[:, 129:130])).astype(BF16)
+        out_ref[0, low_rows, :] = (
+            acc_far[:, :128] / (acc_far[:, 128:129] + acc_far[:, 129:130])
+        ).astype(BF16)
 
 
 def attend(starts, codes, queries, values, keys, enter, head, first, centroids, old):
@@ -459,7 +459,7 @@
         ],
         out_specs=[token, pl.BlockSpec((1, CODES // DPS, HEAD_DIM), lambda h: (h, 0, 0))],
         scratch_shapes=[pltpu.VMEM((CODES, HEAD_DIM), F32)],
-        compiler_params=pltpu.CompilerParams(vmem_limit_bytes=40 << 20),
+        compiler_params=pltpu.CompilerParams(vmem_limit_bytes=60 << 20),
     )(starts, codes, queries, values, keys, enter, head, first, centroids, old)
 
 

time: 187 us -> 168 us (0.90)
  local copies, waits for them, and re-layouts: 12.2 us -> 0 us
  Pallas kernels: 172 us -> 166 us
    unnamed x22 -> x0, local copies, waits for them, and re-layouts: 12.2 us -> none
    pallas_call x1, Pallas kernels: 50 us -> 41 us  [attend(): pl.pallas_call(attend_kernel, name='attend', grid=(HEADS,), out_shape=(ja...]
    pallas_call x1, Pallas kernels: 16.9 us -> 19.6 us  [statistics(): pl.pallas_call(stats_kernel, name='statistics', grid=(HEADS,), out_shape=...]
where the time goes in v2:
time: 168 us; the launch traced here: 166 us
  Pallas kernels  166 us (99%)
    pallas_call x1, Pallas kernels, exchange(): pl.pallas_call(exchange_kernel, name='exchange', out_shape=(jax.ShapeDtyp...  105 us
    pallas_call x1, Pallas kernels, attend(): pl.pallas_call(attend_kernel, name='attend', grid=(HEADS,), out_shape=(ja...  41 us
    pallas_call x1, Pallas kernels, statistics(): pl.pallas_call(stats_kernel, name='statistics', grid=(HEADS,), out_shape=...  19.6 us

profile of v2, /device:TPU:0, one launch (start us, length us, event | category | flops | bytes accessed | tf_op | source)
XLA Modules:
  0.0 166.3 jit_solution(10290246807520824629)
XLA Ops:
  0.6 19.6 %statistics.1 = (f32[8,1032,128]{2,1,0:T(8,128)}, f32[32,264,128]{2,1,0:T(8,128)}, f32[32,264,128]{2,1,0:T(8,128)}, f32[16,8,512]{2,1,0:T(8,128)}) custom-call(s32[1,2]{1,0:T(1,128)} %starts_ref.3, s32[1,16,1024]{2,1,0:T(8,128)} %codes_ref.3, bf16[1,1024,2048]{2,1,0:T(8,128)(2,1)} %k_ref.1, bf16[1,1024,2048]{2,1,0:T(8,128)(2,1)} %v_ref.3), custom_call_target="tpu_custom_call" | custom-call | tf_op jit(solution)/shard_map/statistics/pallas_call | solution.py:92
  20.2 105.1 %exchange.1 = (f32[8,1032,128]{2,1,0:T(8,128)}, f32[32,264,128]{2,1,0:T(8,128)}) custom-call(f32[8,1032,128]{2,1,0:T(8,128)} %get-tuple-element.8.kin, f32[32,264,128]{2,1,0:T(8,128)} %get-tuple-element.9.vin), custom_call_target="tpu_custom_call" | custom-call | tf_op jit(solution)/shard_map/exchange/pallas_call | solution.py:314
  125.4 41.0 %attend.1 = (bf16[1,1024,2048]{2,1,0:T(8,128)(2,1)}, f32[16,128,128]{2,1,0:T(8,128)}) custom-call(s32[1,2]{1,0:T(1,128)} %starts_ref.3, s32[1,16,1024]{2,1,0:T(8,128)} %codes_ref.3, bf16[1,1024,2048]{2,1,0:T(8,128)(2,1)} %q_ref.1, bf16[1,1024,2048]{2,1,0:T(8,128)(2,1)} %v_ref.3, f32[8,1032,128]{2,1,0:T(8,128)} %get-tuple-element.10.keys_ref, ...), custom_call_target="tpu_custom_call" | custom-call | tf_op jit(solution)/shard_map/attend/pallas_call | solution.py:440

commit v3 on v0

v3 whole, which is shorter than its diff:
```python
import jax
import jax.numpy as jnp
from jax import lax
from jax.experimental import pallas as pl
from jax.experimental.pallas import tpu as pltpu
from jax.sharding import PartitionSpec as P

HEADS = 16
HEAD_DIM = 128
CODES = 512
BLOCK = 512
TOK_DEV = 1024
RETAIN = 0.9
NEGATIVE = -1e30
SCORE_TO_LOG2 = 1.4426950408889634 * HEAD_DIM**-0.5

UNIT = 264
GROUPS = 4
F32 = jnp.float32
BF16 = jnp.bfloat16
MESH = pl.DeviceIdType.MESH

(KEY_CORE, VAL_CORE, KEY_Y, VAL_X, KEY_Z, VAL_Z, KEY_X, VAL_BACK, KEY_ZB, KEY_YB, KEY_CB, VAL_CB) = range(12)
PHASES = 12

ATTEND = 25
AT_JOIN = (6, 4)
AT_Y = (14, 3)
AT_SCAN = (14, 3)
AT_Z = (16, 3)
AT_ROWS = (16, 3)
AT_X = (18, 3)
AT_ZB = (20, 3)
AT_SPLIT = (22, 4)
AT_YB = (24, 4)


def column(row):
    return jnp.broadcast_to(row, (128, 128)).T


def head_row(ref, h, lanes, batched):
    tile = pl.ds(pl.multiple_of((h // 8) * 8, 8), 8)
    rows = ref[0, tile, lanes] if batched else ref[tile, lanes]
    picked = lax.broadcasted_iota(jnp.int32, rows.shape, 0) == h % 8
    return jnp.sum(jnp.where(picked, rows, jnp.zeros_like(rows)), axis=0, keepdims=True)


def lanes_of(h):
    return pl.ds(pl.multiple_of(h * HEAD_DIM, HEAD_DIM), HEAD_DIM)


def sum_head(h, starts_ref, codes_ref, keys, values, kin, vin, early_sums, firsts):
    f0 = starts_ref[0, 0].astype(F32)
    f1 = starts_ref[0, 1].astype(F32)
    s1 = 1.0 - f1
    code_iota = lax.broadcasted_iota(jnp.int32, (CODES, BLOCK), 0)
    lane = lax.broadcasted_iota(jnp.int32, (BLOCK, 128), 1).astype(F32)
    place = lax.broadcasted_iota(jnp.int32, (BLOCK, 128), 0).astype(F32)
    sums, counts = [], []
    for b in range(2):
        rows = slice(b * BLOCK, (b + 1) * BLOCK)
        code_row = head_row(codes_ref, h, rows, True)
        hot = jnp.where(code_iota == code_row, 1.0, 0.0).astype(BF16)
        pair = jnp.concatenate([keys[rows, lanes_of(h)], values[rows, lanes_of(h)]], axis=1)
        sums.append(jnp.dot(hot, pair, preferred_element_type=F32))
        code_col = jnp.broadcast_to(code_row.astype(F32), (128, BLOCK)).T
        counted = []
        for r in range(4):
            same = code_col == lane + 128.0 * r
            counted.append(jnp.sum(jnp.where(same, 1.0, 0.0), axis=0, keepdims=True))
            firsts[h, b : b + 1, r * 128 : (r + 1) * 128] = jnp.min(
                jnp.where(same, place, float(BLOCK)), axis=0, keepdims=True
            )
        counts.append(counted)
    flag = jnp.broadcast_to(jnp.maximum(f0, f1), (1, 128))
    none = jnp.zeros((1, 128), F32)
    pad = jnp.zeros((5, 128), F32)
    for g in range(2):
        part = slice(g * 256, (g + 1) * 256)
        at = 2 * h + g
        first = [counts[0][2 * g], counts[0][2 * g + 1]]
        second = [counts[1][2 * g], counts[1][2 * g + 1]]
        both = [first[i] + second[i] for i in range(2)]
        tail = [s1 * first[i] + second[i] for i in range(2)]
        kin[at, 0:256, :] = sums[0][part, :128] + sums[1][part, :128]
        kin[at, 256:264, :] = jnp.concatenate(both + [none, pad], axis=0)
        vin[at, 0:256, :] = s1 * sums[0][part, 128:] + sums[1][part, 128:]
        vin[at, 256:264, :] = jnp.concatenate(tail + [flag, pad], axis=0)
        early_sums[at, 0:256, :] = sums[0][part, 128:]
        early_sums[at, 256:264, :] = jnp.concatenate(first + [flag, pad], axis=0)


def unpacked(ref, h):
    a, b = 2 * h, 2 * h + 1
    sums = jnp.concatenate([ref[a, 0:256, :], ref[b, 0:256, :]], axis=0)
    low, high = ref[a, 256:264, :], ref[b, 256:264, :]
    return sums, [low[0:1], low[1:2], high[0:1], high[1:2]]


def attend_head(
    h, dp, starts_ref, codes_ref, old_ref, queries, values, kout, vout, early_sums, firsts,
    centroids, book_ref, out_ref, share_ref,
):
    alive = [1.0 - starts_ref[0, b].astype(F32) for b in range(2)]
    key_sums, key_counts = unpacked(kout, h)
    for r in range(4):
        rows = slice(r * 128, (r + 1) * 128)
        old = column(head_row(old_ref, h, rows, False))
        now = column(key_counts[r])
        book_ref[rows, :] = (
            RETAIN * old * centroids[rows, :] + (1.0 - RETAIN) * key_sums[rows]
        ) / (RETAIN * old + (1.0 - RETAIN) * now)
    share_ref[...] = book_ref[pl.ds(pl.multiple_of(dp * 128, 128), 128), :]
    book = book_ref[...].astype(BF16)

    sums, counts = unpacked(vout, h)
    counts = jnp.concatenate(counts, axis=1)
    code_iota = lax.broadcasted_iota(jnp.int32, (CODES, BLOCK), 0)
    square_row = lax.broadcasted_iota(jnp.int32, (128, 128), 0)
    ones_column = jnp.where(
        lax.broadcasted_iota(jnp.int32, (BLOCK, 128), 1) == 0, 1.0, 0.0
    ).astype(BF16)
    half = BLOCK // 2
    causal = lax.broadcasted_iota(jnp.int32, (BLOCK, half), 0) >= lax.broadcasted_iota(
        jnp.int32, (BLOCK, half), 1
    )
    place = lax.broadcasted_iota(jnp.int32, (BLOCK, CODES), 0).astype(F32)
    scores_all = lax.dot_general(
        queries[:, lanes_of(h)], book, (((1,), (1,)), ((), ())), preferred_element_type=F32
    )
    for b in range(2):
        if b == 1:
            more, added = unpacked(early_sums, h)
            sums, counts = sums + more, counts + jnp.concatenate(added, axis=1)
        sums, counts = alive[b] * sums, alive[b] * counts
        present = counts > 0
        bias = jnp.where(present, jnp.log2(jnp.maximum(counts, 1.0)), 0.0)
        opens = jnp.where(present, -1.0, firsts[h, b : b + 1, :])
        high = jnp.floor(counts * (1.0 / 256.0)) * 256.0
        low = counts - high
        columns = []
        for r in range(4):
            lanes = slice(r * 128, (r + 1) * 128)
            columns.append(
                jnp.where(
                    square_row == 0, high[:, lanes], jnp.where(square_row == 1, low[:, lanes], 0.0)
                ).T
            )
        cache = jnp.concatenate([sums, jnp.concatenate(columns, axis=0)], axis=1).astype(BF16)
        rows = slice(b * BLOCK, (b + 1) * BLOCK)
        code_row = head_row(codes_ref, h, rows, True)
        hot = jnp.where(code_iota == code_row, 1.0, 0.0).astype(BF16)
        local = jnp.concatenate([values[rows, lanes_of(h)], ones_column], axis=1)
        scores = scores_all[rows] * SCORE_TO_LOG2
        top = jnp.max(jnp.where(opens <= place, scores + bias, NEGATIVE), axis=1, keepdims=True)
        weight = jnp.exp2(jnp.minimum(scores - top, 0.0)).astype(BF16)
        near = jnp.dot(weight, hot[:, :half], preferred_element_type=F32)
        near = jnp.where(causal, near, 0.0).astype(BF16)
        far = jnp.dot(weight[half:], hot[:, half:], preferred_element_type=F32)
        far = jnp.where(causal[:half], far, 0.0).astype(BF16)
        acc = jnp.dot(weight, cache, preferred_element_type=F32)
        acc = acc + jnp.dot(near, local[:half], preferred_element_type=F32)
        acc_far = acc[half:] + jnp.dot(far, local[half:], preferred_element_type=F32)
        acc = acc[:half]
        top_rows = slice(b * BLOCK, b * BLOCK + half)
        low_rows = slice(b * BLOCK + half, (b + 1) * BLOCK)
        out_ref[top_rows, :] = (acc[:, :128] / (acc[:, 128:129] + acc[:, 129:130])).astype(BF16)
        out_ref[low_rows, :] = (
            acc_far[:, :128] / (acc_far[:, 128:129] + acc_far[:, 129:130])
        ).astype(BF16)


def layer_kernel(
    starts_ref, codes_ref, old_ref, q_hbm, k_hbm, v_hbm, cent_hbm, out_hbm, book_hbm,
    kq, values, cents, book_ref, outs, shares, firsts, kin, vin, early_sums, kout, vout,
    kc, vc, ky, s1, kz, xsrc, kx, own, vchip, vx, vz, v2, back,
    k_sem, v_sem, q_sem, cent_sem, out_sem, share_sem, send, recv,
):
    y = lax.axis_index("dp")
    me = lax.axis_index("seq")
    c = me % 2
    x = (me // 2) % 4
    z = me // 8

    def at(dz=0, dx=0, dc=0):
        return {"seq": (((z + dz) % 4) * 4 + (x + dx) % 4) * 2 + (c + dc) % 2}

    def at_y(dy):
        return {"dp": (y + dy) % 4}

    def remote(src, dst, phase, g, device):
        return pltpu.make_async_remote_copy(
            src_ref=src, dst_ref=dst, send_sem=send.at[phase, g], recv_sem=recv.at[phase, g],
            device_id=device, device_id_type=MESH,
        )

    def four(g):
        return vchip.at[g]

    def three(g):
        return vchip.at[g, pl.ds(0, 3)]

    def three_slices(g):
        return s1.at[g, pl.ds(0, 3)]

    def three_rows(g):
        return vchip.at[g, 0, pl.ds(0, 192)]

    sizes = {
        KEY_CORE: four, VAL_CORE: four, KEY_Y: three, VAL_X: three, KEY_Z: three_slices,
        VAL_Z: three, KEY_X: three_slices, VAL_BACK: three, KEY_ZB: three_rows, KEY_YB: three,
        KEY_CB: four, VAL_CB: four,
    }

    def arrived(phase, g):
        part = sizes[phase](g)
        remote(part, part, phase, g, at(dc=1)).wait_recv()

    def left(phase, g):
        part = sizes[phase](g)
        remote(part, part, phase, g, at(dc=1)).wait_send()

    def unit_loop(body):
        def step(u, carry):
            body(u)
            return carry

        lax.fori_loop(0, 4, step, 0)

    def columns_of(g):
        return pl.ds(pl.multiple_of(g * 512, 512), 512)

    def load_keys(g):
        return pltpu.make_async_copy(k_hbm.at[0, :, columns_of(g)], kq.at[:, columns_of(g)], k_sem.at[g])

    def load_values(g):
        return pltpu.make_async_copy(v_hbm.at[0, :, columns_of(g)], values.at[:, columns_of(g)], v_sem.at[g])

    def load_queries():
        return pltpu.make_async_copy(q_hbm.at[0], kq, q_sem)

    def load_centroids(h):
        return pltpu.make_async_copy(cent_hbm.at[h], cents.at[h % 2], cent_sem.at[h % 2])

    def store_out(h):
        return pltpu.make_async_copy(outs.at[h % 2], out_hbm.at[0, :, lanes_of(h)], out_sem.at[h % 2])

    def store_share(h):
        return pltpu.make_async_copy(shares.at[h % 2], book_hbm.at[h], share_sem.at[h % 2])

    for g in range(GROUPS):
        load_keys(g).start()
        load_values(g).start()
    for h in range(2):
        load_centroids(h).start()

    barrier = pltpu.get_barrier_semaphore()

    def greet(device):
        pl.semaphore_signal(barrier, inc=1, device_id=device, device_id_type=MESH)

    greet(at(dc=1))
    for k in (1, 2, 3):
        greet(at(dx=k))
        greet(at(dz=k))
        greet(at_y(k))
    pl.semaphore_wait(barrier, 10)

    def share_cores(g):
        theirs = pl.ds(8 * g + 4 * (1 - c), 4)
        remote(kin.at[theirs], kc.at[g], KEY_CORE, g, at(dc=1)).start()
        remote(vin.at[theirs], vc.at[g], VAL_CORE, g, at(dc=1)).start()

    def join(g):
        mine = 8 * g + 4 * c
        arrived(KEY_CORE, g)

        def add(u):
            kc[g, u] = kc[g, u] + kin[mine + u]

        unit_loop(add)
        for k in (1, 2, 3):
            remote(kc.at[g, (y + k) % 4], ky.at[g, 3 - k], KEY_Y, g, at_y(k)).start()
        arrived(VAL_CORE, g)

        def link(u):
            ours = vin[mine + u]
            theirs = vc[g, u]
            early = jnp.where(c == 0, ours, theirs)
            late = jnp.where(c == 0, theirs, ours)
            vchip[g, u] = late + (1.0 - late[258:259, :]) * early

        unit_loop(link)
        for k in (1, 2, 3):
            remote(vchip.at[g, (x + k) % 4], vx.at[g, x], VAL_X, g, at(dx=k)).start()
        vx[g, x] = vchip[g, x]

    def keys_y(g):
        arrived(KEY_Y, g)

        def add(i):
            rows = pl.ds(pl.multiple_of(i * 64, 64), 64)
            s1[g, i, 0:64, :] = (kc[g, y, rows, :] + ky[g, 0, rows, :]) + (
                ky[g, 1, rows, :] + ky[g, 2, rows, :]
            )
            s1[g, i, 64:72, :] = (kc[g, y, 256:264, :] + ky[g, 0, 256:264, :]) + (
                ky[g, 1, 256:264, :] + ky[g, 2, 256:264, :]
            )

        unit_loop(add)
        for k in (1, 2, 3):
            remote(s1.at[g, (z + k) % 4], kz.at[g, 3 - k], KEY_Z, g, at(dz=k)).start()

    def keys_z(g):
        arrived(KEY_Z, g)
        part = (s1[g, z] + kz[g, 0]) + (kz[g, 1] + kz[g, 2])
        xsrc[g] = part
        kx[g, x] = part
        for k in (1, 2, 3):
            remote(xsrc.at[g], kx.at[g, x], KEY_X, g, at(dx=k)).start()

    def slice_of_unit():
        return pl.ds(pl.multiple_of(z * 64, 64), 64)

    def keys_x(g):
        arrived(KEY_X, g)
        total = (kx[g, 0] + kx[g, 1]) + (kx[g, 2] + kx[g, 3])
        unit = 8 * g + 4 * c + y
        own[g] = total[0:64]
        kout[unit, slice_of_unit(), :] = total[0:64]
        kout[unit, 256:264, :] = total[64:72]
        for k in (1, 2, 3):
            remote(own.at[g], kout.at[unit, slice_of_unit()], KEY_ZB, g, at(dz=k)).start()

    def keys_back_z(g):
        arrived(KEY_ZB, g)
        unit = kout.at[8 * g + 4 * c + y]
        for k in (1, 2, 3):
            remote(unit, unit, KEY_YB, g, at_y(k)).start()

    def keys_back_y(g):
        arrived(KEY_YB, g)
        mine = kout.at[pl.ds(8 * g + 4 * c, 4)]
        remote(mine, mine, KEY_CB, g, at(dc=1)).start()

    def scan_row(g):
        arrived(VAL_X, g)

        def step(j, run):
            part = vx[g, j]
            vx[g, j] = run
            return part + (1.0 - part[258:259, :]) * run

        vz[g, z] = lax.fori_loop(0, 4, step, jnp.zeros((UNIT, 128), F32))
        for k in (1, 2, 3):
            remote(vz.at[g, z], vz.at[g, z], VAL_Z, g, at(dz=k)).start()

    def scan_rows(g):
        arrived(VAL_Z, g)

        def step(j, run):
            part = vz[g, j]
            return jnp.where(j < z, part + (1.0 - part[258:259, :]) * run, run)

        ahead = lax.fori_loop(0, 3, step, jnp.zeros((UNIT, 128), F32))

        def enter(j):
            part = vx[g, j]
            vx[g, j] = part + (1.0 - part[258:259, :]) * ahead

        unit_loop(enter)
        for k in (1, 2, 3):
            remote(vx.at[g, (x + k) % 4], v2.at[g, x], VAL_BACK, g, at(dx=k)).start()
        v2[g, x] = vx[g, x]

    def split(g):
        arrived(VAL_BACK, g)
        mine = 8 * g + 4 * c

        def part(u):
            early = jnp.where(c == 0, vin[mine + u], vc[g, u])
            first = v2[g, u]
            second = early + (1.0 - early[258:259, :]) * first
            vout[mine + u] = jnp.where(c == 0, first, second)
            back[g, u] = jnp.where(c == 0, second, first)

        unit_loop(part)
        remote(back.at[g], vout.at[pl.ds(mine, 4)], VAL_CB, g, at(dc=1)).start()

    def step(tick, carry):
        @pl.when(tick < HEADS)
        def _():
            h = tick
            g = h // 4

            @pl.when(h % 4 == 0)
            def _():
                load_keys(g).wait()
                load_values(g).wait()

            sum_head(h, starts_ref, codes_ref, kq, values, kin, vin, early_sums, firsts)

            @pl.when(h % 4 == 3)
            def _():
                share_cores(g)

            @pl.when(h == HEADS - 1)
            def _():
                load_queries().start()

        @pl.when(tick >= ATTEND)
        def _():
            h = tick - ATTEND
            g = h // 4

            @pl.when(h == 0)
            def _():
                load_queries().wait()

            @pl.when(h % 4 == 0)
            def _():
                arrived(KEY_CB, g)
                arrived(VAL_CB, g)

            load_centroids(h).wait()

            @pl.when(h >= 2)
            def _():
                store_out(h - 2).wait()
                store_share(h - 2).wait()

            attend_head(
                h, y, starts_ref, codes_ref, old_ref, kq, values, kout, vout, early_sums, firsts,
                cents.at[h % 2], book_ref, outs.at[h % 2], shares.at[h % 2],
            )
            store_out(h).start()
            store_share(h).start()

            @pl.when(h + 2 < HEADS)
            def _():
                load_centroids(h + 2).start()

        for when, stage in (
            (AT_YB, keys_back_y), (AT_SPLIT, split), (AT_ZB, keys_back_z), (AT_X, keys_x),
            (AT_Z, keys_z), (AT_ROWS, scan_rows), (AT_Y, keys_y), (AT_SCAN, scan_row),
            (AT_JOIN, join),
        ):
            first, stride = when
            since = tick - first

            @pl.when((since >= 0) & (since % stride == 0) & (since < GROUPS * stride))
            def _(stage=stage, since=since, stride=stride):
                stage(since // stride)

        return carry

    lax.fori_loop(0, ATTEND + HEADS, step, 0)

    for h in (HEADS - 2, HEADS - 1):
        store_out(h).wait()
        store_share(h).wait()

    def finish(g, carry):
        for phase in range(PHASES):
            left(phase, g)
        return carry

    lax.fori_loop(0, GROUPS, finish, 0)


def layer(queries, keys, values, codes, starts, centroids, old):
    anywhere = pl.BlockSpec(memory_space=pl.ANY)
    whole = pl.BlockSpec(memory_space=pltpu.VMEM)

    def units(*shape):
        return pltpu.VMEM((*shape, 128), F32)

    return pl.pallas_call(
        layer_kernel,
        name="layer",
        out_shape=(
            jax.ShapeDtypeStruct((1, TOK_DEV, HEADS * HEAD_DIM), BF16),
            jax.ShapeDtypeStruct((HEADS, CODES // 4, HEAD_DIM), F32),
        ),
        in_specs=[pl.BlockSpec(memory_space=pltpu.SMEM), whole, whole] + [anywhere] * 4,
        out_specs=[anywhere, anywhere],
        scratch_shapes=[
            pltpu.VMEM((TOK_DEV, HEADS * HEAD_DIM), BF16),
            pltpu.VMEM((TOK_DEV, HEADS * HEAD_DIM), BF16),
            units(2, CODES),
            units(CODES),
            pltpu.VMEM((2, TOK_DEV, HEAD_DIM), BF16),
            units(2, CODES // 4),
            pltpu.VMEM((HEADS, 8, CODES), F32),
            units(32, UNIT),
            units(32, UNIT),
            units(32, UNIT),
            units(32, UNIT),
            units(32, UNIT),
            units(GROUPS, 4, UNIT),
            units(GROUPS, 4, UNIT),
            units(GROUPS, 3, UNIT),
            units(GROUPS, 4, 72),
            units(GROUPS, 3, 72),
            units(GROUPS, 72),
            units(GROUPS, 4, 72),
            units(GROUPS, 64),
            units(GROUPS, 4, UNIT),
            units(GROUPS, 4, UNIT),
            units(GROUPS, 4, UNIT),
            units(GROUPS, 4, UNIT),
            units(GROUPS, 4, UNIT),
            pltpu.SemaphoreType.DMA((GROUPS,)),
            pltpu.SemaphoreType.DMA((GROUPS,)),
            pltpu.SemaphoreType.DMA,
            pltpu.SemaphoreType.DMA((2,)),
            pltpu.SemaphoreType.DMA((2,)),
            pltpu.SemaphoreType.DMA((2,)),
            pltpu.SemaphoreType.DMA((PHASES, GROUPS)),
            pltpu.SemaphoreType.DMA((PHASES, GROUPS)),
        ],
        compiler_params=pltpu.CompilerParams(
            collective_id=0, has_side_effects=True, vmem_limit_bytes=63 << 20
        ),
    )(starts, codes, old, queries, keys, values, centroids)


def shards(queries, keys, values, codes, starts, old_centroids, old_counts):
    return layer(queries, keys, values, codes, starts, old_centroids, old_counts)


def solution(mesh):
    placed = (
        P("dp", "seq", None),
        P("dp", "seq", None),
        P("dp", "seq", None),
        P("dp", None, "seq"),
        P("dp", "seq"),
        P(),
        P(),
    )
    return jax.shard_map(
        shards,
        mesh=mesh,
        in_specs=placed,
        out_specs=(P("dp", "seq", None), P(None, "dp", None)),
        check_vma=False,
    )
```

time: 887 us -> 115 us (0.13)
  the two profiles are of different devices: /device:TPU:103 before, /device:TPU:1 now
where the time goes in v3:
time: 115 us
  Pallas kernels  108 us (94%)
  local copies, waits for them, and re-layouts  5.85 us (5%)
    pallas_call x1, Pallas kernels, layer(): pl.pallas_call(layer_kernel, name='layer', out_shape=(jax.ShapeDtypeStruc...  108 us
    unnamed x4, local copies, waits for them, and re-layouts  5.85 us

profile of v3, /device:TPU:1, one launch (start us, length us, event | category | flops | bytes accessed | tf_op | source)
XLA Modules:
  0.0 114.6 jit_solution(6644919848010988059)
XLA Ops:
  0.6 108.1 %layer.1 = (bf16[1,1024,2048]{2,1,0:T(8,128)(2,1)}, f32[16,128,128]{2,1,0:T(8,128)}) custom-call(s32[1,2]{1,0:T(1,128)} %starts_ref.1, s32[1,16,1024]{2,1,0:T(8,128)} %codes_ref.1, f32[16,512]{1,0:T(8,128)} %old_ref.1, bf16[1,1024,2048]{2,1,0:T(8,128)(2,1)} %q_hbm.1, bf16[1,1024,2048]{2,1,0:T(8,128)(2,1)} %k_hbm.1, bf16[1,1024,2048]{2,1,0:T(8,128)(2,1)} %v_hbm.1, ...), custom_call_target="tpu_custom_call" | custom-call | tf_op jit(solution)/shard_map/layer/pallas_call | solution.py:479
  108.8 0.0 copy-start
  108.8 4.9 %copy.11 = bf16[1,1024,2048]{2,1,0:T(8,128)(2,1)} copy(bf16[1,1024,2048]{2,1,0:T(8,128)(2,1)} %get-tuple-element.4) | data formatting | bytes 8388608
  113.7 0.0 copy-done
  113.7 1.0 copy.12
Async XLA Ops:
  108.8 4.9 %copy-start = (f32[16,128,128]{2,1,0:T(8,128)S(1)}, f32[16,128,128]{2,1,0:T(8,128)}, u32[]{:S(2)}) copy-start(f32[16,128,128]{2,1,0:T(8,128)} %get-tuple-element.5) | copy-start | bytes 3145732

commit v4 on v3

--- a/solution.py
+++ b/solution.py
@@ -14,8 +14,12 @@
 NEGATIVE = -1e30
 SCORE_TO_LOG2 = 1.4426950408889634 * HEAD_DIM**-0.5
 
-UNIT = 264
-GROUPS = 4
+UNIT = 136
+UNITS = 64
+GROUPS = 8
+PER_GROUP = 2
+PART = 32
+SLICE = PART + 8
 F32 = jnp.float32
 BF16 = jnp.bfloat16
 MESH = pl.DeviceIdType.MESH
@@ -23,16 +27,16 @@
 (KEY_CORE, VAL_CORE, KEY_Y, VAL_X, KEY_Z, VAL_Z, KEY_X, VAL_BACK, KEY_ZB, KEY_YB, KEY_CB, VAL_CB) = range(12)
 PHASES = 12
 
-ATTEND = 25
-AT_JOIN = (6, 4)
-AT_Y = (14, 3)
-AT_SCAN = (14, 3)
-AT_Z = (16, 3)
-AT_ROWS = (16, 3)
-AT_X = (18, 3)
-AT_ZB = (20, 3)
-AT_SPLIT = (22, 4)
-AT_YB = (24, 4)
+ATTEND = 16
+AT_JOIN = (3, 2)
+AT_Y = (6, 2)
+AT_SCAN = (7, 2)
+AT_Z = (8, 2)
+AT_ROWS = (10, 2)
+AT_X = (11, 2)
+AT_ZB = (12, 2)
+AT_SPLIT = (14, 2)
+AT_YB = (14, 2)
 
 
 def column(row):
@@ -75,27 +79,22 @@
         counts.append(counted)
     flag = jnp.broadcast_to(jnp.maximum(f0, f1), (1, 128))
     none = jnp.zeros((1, 128), F32)
-    pad = jnp.zeros((5, 128), F32)
-    for g in range(2):
-        part = slice(g * 256, (g + 1) * 256)
-        at = 2 * h + g
-        first = [counts[0][2 * g], counts[0][2 * g + 1]]
-        second = [counts[1][2 * g], counts[1][2 * g + 1]]
-        both = [first[i] + second[i] for i in range(2)]
-        tail = [s1 * first[i] + second[i] for i in range(2)]
-        kin[at, 0:256, :] = sums[0][part, :128] + sums[1][part, :128]
-        kin[at, 256:264, :] = jnp.concatenate(both + [none, pad], axis=0)
-        vin[at, 0:256, :] = s1 * sums[0][part, 128:] + sums[1][part, 128:]
-        vin[at, 256:264, :] = jnp.concatenate(tail + [flag, pad], axis=0)
-        early_sums[at, 0:256, :] = sums[0][part, 128:]
-        early_sums[at, 256:264, :] = jnp.concatenate(first + [flag, pad], axis=0)
+    pad = jnp.zeros((6, 128), F32)
+    for i in range(4):
+        part = slice(i * 128, (i + 1) * 128)
+        at = 4 * h + i
+        first, second = counts[0][i], counts[1][i]
+        kin[at, 0:128, :] = sums[0][part, :128] + sums[1][part, :128]
+        kin[at, 128:136, :] = jnp.concatenate([first + second, none, pad], axis=0)
+        vin[at, 0:128, :] = s1 * sums[0][part, 128:] + sums[1][part, 128:]
+        vin[at, 128:136, :] = jnp.concatenate([s1 * first + second, flag, pad], axis=0)
+        early_sums[at, 0:128, :] = sums[0][part, 128:]
+        early_sums[at, 128:136, :] = jnp.concatenate([first, flag, pad], axis=0)
 
 
 def unpacked(ref, h):
-    a, b = 2 * h, 2 * h + 1
-    sums = jnp.concatenate([ref[a, 0:256, :], ref[b, 0:256, :]], axis=0)
-    low, high = ref[a, 256:264, :], ref[b, 256:264, :]
-    return sums, [low[0:1], low[1:2], high[0:1], high[1:2]]
+    sums = jnp.concatenate([ref[4 * h + i, 0:128, :] for i in range(4)], axis=0)
+    return sums, [ref[4 * h + i, 128:136, :][0:1] for i in range(4)]
 
 
 def attend_head(
@@ -205,7 +204,7 @@
         return s1.at[g, pl.ds(0, 3)]
 
     def three_rows(g):
-        return vchip.at[g, 0, pl.ds(0, 192)]
+        return vchip.at[g, 0, pl.ds(0, 3 * PART)]
 
     sizes = {
         KEY_CORE: four, VAL_CORE: four, KEY_Y: three, VAL_X: three, KEY_Z: three_slices,
@@ -229,7 +228,7 @@
         lax.fori_loop(0, 4, step, 0)
 
     def columns_of(g):
-        return pl.ds(pl.multiple_of(g * 512, 512), 512)
+        return pl.ds(pl.multiple_of(g * 256, 256), 256)
 
     def load_keys(g):
         return pltpu.make_async_copy(k_hbm.at[0, :, columns_of(g)], kq.at[:, columns_of(g)], k_sem.at[g])
@@ -289,7 +288,7 @@
             theirs = vc[g, u]
             early = jnp.where(c == 0, ours, theirs)
             late = jnp.where(c == 0, theirs, ours)
-            vchip[g, u] = late + (1.0 - late[258:259, :]) * early
+            vchip[g, u] = late + (1.0 - late[129:130, :]) * early
 
         unit_loop(link)
         for k in (1, 2, 3):
@@ -300,12 +299,12 @@
         arrived(KEY_Y, g)
 
         def add(i):
-            rows = pl.ds(pl.multiple_of(i * 64, 64), 64)
-            s1[g, i, 0:64, :] = (kc[g, y, rows, :] + ky[g, 0, rows, :]) + (
+            rows = pl.ds(pl.multiple_of(i * PART, PART), PART)
+            s1[g, i, 0:PART, :] = (kc[g, y, rows, :] + ky[g, 0, rows, :]) + (
                 ky[g, 1, rows, :] + ky[g, 2, rows, :]
             )
-            s1[g, i, 64:72, :] = (kc[g, y, 256:264, :] + ky[g, 0, 256:264, :]) + (
-                ky[g, 1, 256:264, :] + ky[g, 2, 256:264, :]
+            s1[g, i, PART:SLICE, :] = (kc[g, y, 128:136, :] + ky[g, 0, 128:136, :]) + (
+                ky[g, 1, 128:136, :] + ky[g, 2, 128:136, :]
             )
 
         unit_loop(add)
@@ -321,15 +320,15 @@
             remote(xsrc.at[g], kx.at[g, x], KEY_X, g, at(dx=k)).start()
 
     def slice_of_unit():
-        return pl.ds(pl.multiple_of(z * 64, 64), 64)
+        return pl.ds(pl.multiple_of(z * PART, PART), PART)
 
     def keys_x(g):
         arrived(KEY_X, g)
         total = (kx[g, 0] + kx[g, 1]) + (kx[g, 2] + kx[g, 3])
         unit = 8 * g + 4 * c + y
-        own[g] = total[0:64]
-        kout[unit, slice_of_unit(), :] = total[0:64]
-        kout[unit, 256:264, :] = total[64:72]
+        own[g] = total[0:PART]
+        kout[unit, slice_of_unit(), :] = total[0:PART]
+        kout[unit, 128:136, :] = total[PART:SLICE]
         for k in (1, 2, 3):
             remote(own.at[g], kout.at[unit, slice_of_unit()], KEY_ZB, g, at(dz=k)).start()
 
@@ -350,7 +349,7 @@
         def step(j, run):
             part = vx[g, j]
             vx[g, j] = run
-            return part + (1.0 - part[258:259, :]) * run
+            return part + (1.0 - part[129:130, :]) * run
 
         vz[g, z] = lax.fori_loop(0, 4, step, jnp.zeros((UNIT, 128), F32))
         for k in (1, 2, 3):
@@ -361,13 +360,13 @@
 
         def step(j, run):
             part = vz[g, j]
-            return jnp.where(j < z, part + (1.0 - part[258:259, :]) * run, run)
+            return jnp.where(j < z, part + (1.0 - part[129:130, :]) * run, run)
 
         ahead = lax.fori_loop(0, 3, step, jnp.zeros((UNIT, 128), F32))
 
         def enter(j):
             part = vx[g, j]
-            vx[g, j] = part + (1.0 - part[258:259, :]) * ahead
+            vx[g, j] = part + (1.0 - part[129:130, :]) * ahead
 
         unit_loop(enter)
         for k in (1, 2, 3):
@@ -381,7 +380,7 @@
         def part(u):
             early = jnp.where(c == 0, vin[mine + u], vc[g, u])
             first = v2[g, u]
-            second = early + (1.0 - early[258:259, :]) * first
+            second = early + (1.0 - early[129:130, :]) * first
             vout[mine + u] = jnp.where(c == 0, first, second)
             back[g, u] = jnp.where(c == 0, second, first)
 
@@ -392,16 +391,16 @@
         @pl.when(tick < HEADS)
         def _():
             h = tick
-            g = h // 4
-
-            @pl.when(h % 4 == 0)
+            g = h // PER_GROUP
+
+            @pl.when(h % PER_GROUP == 0)
             def _():
                 load_keys(g).wait()
                 load_values(g).wait()
 
             sum_head(h, starts_ref, codes_ref, kq, values, kin, vin, early_sums, firsts)
 
-            @pl.when(h % 4 == 3)
+            @pl.when(h % PER_GROUP == PER_GROUP - 1)
             def _():
                 share_cores(g)
 
@@ -412,13 +411,13 @@
         @pl.when(tick >= ATTEND)
         def _():
             h = tick - ATTEND
-            g = h // 4
+            g = h // PER_GROUP
 
             @pl.when(h == 0)
             def _():
                 load_queries().wait()
 
-            @pl.when(h % 4 == 0)
+            @pl.when(h % PER_GROUP == 0)
             def _():
                 arrived(KEY_CB, g)
                 arrived(VAL_CB, g)
@@ -493,19 +492,19 @@
             pltpu.VMEM((2, TOK_DEV, HEAD_DIM), BF16),
             units(2, CODES // 4),
             pltpu.VMEM((HEADS, 8, CODES), F32),
-            units(32, UNIT),
-            units(32, UNIT),
-            units(32, UNIT),
-            units(32, UNIT),
-            units(32, UNIT),
+            units(UNITS, UNIT),
+            units(UNITS, UNIT),
+            units(UNITS, UNIT),
+            units(UNITS, UNIT),
+            units(UNITS, UNIT),
             units(GROUPS, 4, UNIT),
             units(GROUPS, 4, UNIT),
             units(GROUPS, 3, UNIT),
-            units(GROUPS, 4, 72),
-            units(GROUPS, 3, 72),
-            units(GROUPS, 72),
-            units(GROUPS, 4, 72),
-            units(GROUPS, 64),
+            units(GROUPS, 4, SLICE),
+            units(GROUPS, 3, SLICE),
+            units(GROUPS, SLICE),
+            units(GROUPS, 4, SLICE),
+            units(GROUPS, PART),
             units(GROUPS, 4, UNIT),
             units(GROUPS, 4, UNIT),
             units(GROUPS, 4, UNIT),

time: 115 us -> 96.2 us (0.84)
  the two profiles are of different devices: /device:TPU:1 before, /device:TPU:0 now
where the time goes in v4:
time: 96.2 us; the launch traced here: 95.9 us
  Pallas kernels  89.4 us (93%)
  local copies, waits for them, and re-layouts  5.85 us (6%)
    pallas_call x1, Pallas kernels, layer(): pl.pallas_call(layer_kernel, name='layer', out_shape=(jax.ShapeDtypeStruc...  89.4 us
    unnamed x4, local copies, waits for them, and re-layouts  5.85 us

profile of v4, /device:TPU:0, one launch (start us, length us, event | category | flops | bytes accessed | tf_op | source)
XLA Modules:
  0.0 95.9 jit_solution(12374642241423030591)
XLA Ops:
  0.6 89.4 %layer.1 = (bf16[1,1024,2048]{2,1,0:T(8,128)(2,1)}, f32[16,128,128]{2,1,0:T(8,128)}) custom-call(s32[1,2]{1,0:T(1,128)} %starts_ref.1, s32[1,16,1024]{2,1,0:T(8,128)} %codes_ref.1, f32[16,512]{1,0:T(8,128)} %old_ref.1, bf16[1,1024,2048]{2,1,0:T(8,128)(2,1)} %q_hbm.1, bf16[1,1024,2048]{2,1,0:T(8,128)(2,1)} %k_hbm.1, bf16[1,1024,2048]{2,1,0:T(8,128)(2,1)} %v_hbm.1, ...), custom_call_target="tpu_custom_call" | custom-call | tf_op jit(solution)/shard_map/layer/pallas_call | solution.py:478
  90.0 0.0 copy-start
  90.0 4.9 %copy.11 = bf16[1,1024,2048]{2,1,0:T(8,128)(2,1)} copy(bf16[1,1024,2048]{2,1,0:T(8,128)(2,1)} %get-tuple-element.4) | data formatting | bytes 8388608
  94.9 0.0 copy-done
  94.9 1.0 %copy.12 = f32[16,128,128]{2,1,0:T(8,128)} copy(f32[16,128,128]{2,1,0:T(8,128)S(1)} %copy-done) | data formatting | bytes 2097152
Async XLA Ops:
  90.0 4.9 %copy-start = (f32[16,128,128]{2,1,0:T(8,128)S(1)}, f32[16,128,128]{2,1,0:T(8,128)}, u32[]{:S(2)}) copy-start(f32[16,128,128]{2,1,0:T(8,128)} %get-tuple-element.5) | copy-start | bytes 3145732

commit v5 on v4

--- a/solution.py
+++ b/solution.py
@@ -27,16 +27,23 @@
 (KEY_CORE, VAL_CORE, KEY_Y, VAL_X, KEY_Z, VAL_Z, KEY_X, VAL_BACK, KEY_ZB, KEY_YB, KEY_CB, VAL_CB) = range(12)
 PHASES = 12
 
-ATTEND = 16
-AT_JOIN = (3, 2)
-AT_Y = (6, 2)
-AT_SCAN = (7, 2)
-AT_Z = (8, 2)
-AT_ROWS = (10, 2)
-AT_X = (11, 2)
-AT_ZB = (12, 2)
-AT_SPLIT = (14, 2)
-AT_YB = (14, 2)
+ATTEND = 9
+AT_JOIN = (1, 2, 3, 4, 5, 6, 7, 8)
+AT_Y = (3, 4, 5, 6, 6, 7, 8, 9)
+AT_SCAN = (3, 4, 5, 7, 7, 8, 10, 10)
+AT_Z = (4, 5, 6, 7, 7, 8, 10, 10)
+AT_ROWS = (5, 6, 7, 8, 9, 10, 11, 12)
+AT_X = (5, 6, 7, 8, 8, 10, 11, 11)
+AT_ZB = (6, 7, 8, 9, 9, 11, 12, 12)
+AT_SPLIT = (7, 8, 9, 10, 11, 12, 13, 14)
+AT_YB = (7, 8, 9, 10, 11, 12, 13, 14)
+
+
+def groups_before(when, tick):
+    count = 0
+    for at in when:
+        count = count + jnp.minimum(jnp.maximum(tick - at, 0), 1)
+    return count
 
 
 def column(row):
@@ -58,14 +65,14 @@
     f0 = starts_ref[0, 0].astype(F32)
     f1 = starts_ref[0, 1].astype(F32)
     s1 = 1.0 - f1
-    code_iota = lax.broadcasted_iota(jnp.int32, (CODES, BLOCK), 0)
+    code_iota = lax.broadcasted_iota(jnp.int16, (CODES, BLOCK), 0)
     lane = lax.broadcasted_iota(jnp.int32, (BLOCK, 128), 1).astype(F32)
     place = lax.broadcasted_iota(jnp.int32, (BLOCK, 128), 0).astype(F32)
     sums, counts = [], []
     for b in range(2):
         rows = slice(b * BLOCK, (b + 1) * BLOCK)
         code_row = head_row(codes_ref, h, rows, True)
-        hot = jnp.where(code_iota == code_row, 1.0, 0.0).astype(BF16)
+        hot = jnp.where(code_iota == code_row.astype(jnp.int16), jnp.ones((), BF16), jnp.zeros((), BF16))
         pair = jnp.concatenate([keys[rows, lanes_of(h)], values[rows, lanes_of(h)]], axis=1)
         sums.append(jnp.dot(hot, pair, preferred_element_type=F32))
         code_col = jnp.broadcast_to(code_row.astype(F32), (128, BLOCK)).T
@@ -121,13 +128,20 @@
         lax.broadcasted_iota(jnp.int32, (BLOCK, 128), 1) == 0, 1.0, 0.0
     ).astype(BF16)
     half = BLOCK // 2
-    causal = lax.broadcasted_iota(jnp.int32, (BLOCK, half), 0) >= lax.broadcasted_iota(
-        jnp.int32, (BLOCK, half), 1
+    causal = lax.broadcasted_iota(jnp.int32, (half, half), 0) >= lax.broadcasted_iota(
+        jnp.int32, (half, half), 1
     )
     place = lax.broadcasted_iota(jnp.int32, (BLOCK, CODES), 0).astype(F32)
-    scores_all = lax.dot_general(
-        queries[:, lanes_of(h)], book, (((1,), (1,)), ((), ())), preferred_element_type=F32
-    )
+    block_scores = [
+        lax.dot_general(
+            queries[b * BLOCK : (b + 1) * BLOCK, lanes_of(h)],
+            book,
+            (((1,), (1,)), ((), ())),
+            preferred_element_type=F32,
+        )
+        for b in range(2)
+    ]
+    weights, picks, tables = [], [], []
     for b in range(2):
         if b == 1:
             more, added = unpacked(early_sums, h)
@@ -151,23 +165,23 @@
         code_row = head_row(codes_ref, h, rows, True)
         hot = jnp.where(code_iota == code_row, 1.0, 0.0).astype(BF16)
         local = jnp.concatenate([values[rows, lanes_of(h)], ones_column], axis=1)
-        scores = scores_all[rows] * SCORE_TO_LOG2
+        scores = block_scores[b] * SCORE_TO_LOG2
         top = jnp.max(jnp.where(opens <= place, scores + bias, NEGATIVE), axis=1, keepdims=True)
-        weight = jnp.exp2(jnp.minimum(scores - top, 0.0)).astype(BF16)
+        weights.append(jnp.exp2(jnp.minimum(scores - top, 0.0)).astype(BF16))
+        picks.append(hot)
+        tables.append(jnp.concatenate([cache, local], axis=0))
+    for b in range(2):
+        weight, hot, table = weights[b], picks[b], tables[b]
         near = jnp.dot(weight, hot[:, :half], preferred_element_type=F32)
-        near = jnp.where(causal, near, 0.0).astype(BF16)
         far = jnp.dot(weight[half:], hot[:, half:], preferred_element_type=F32)
-        far = jnp.where(causal[:half], far, 0.0).astype(BF16)
-        acc = jnp.dot(weight, cache, preferred_element_type=F32)
-        acc = acc + jnp.dot(near, local[:half], preferred_element_type=F32)
-        acc_far = acc[half:] + jnp.dot(far, local[half:], preferred_element_type=F32)
-        acc = acc[:half]
-        top_rows = slice(b * BLOCK, b * BLOCK + half)
-        low_rows = slice(b * BLOCK + half, (b + 1) * BLOCK)
-        out_ref[top_rows, :] = (acc[:, :128] / (acc[:, 128:129] + acc[:, 129:130])).astype(BF16)
-        out_ref[low_rows, :] = (
-            acc_far[:, :128] / (acc_far[:, 128:129] + acc_far[:, 129:130])
-        ).astype(BF16)
+        local_first = jnp.where(causal, near[:half], 0.0).astype(BF16)
+        local_second = [near[half:].astype(BF16), jnp.where(causal, far, 0.0).astype(BF16)]
+        upper = jnp.concatenate([weight[:half], local_first], axis=1)
+        lower = jnp.concatenate([weight[half:]] + local_second, axis=1)
+        for i, part in enumerate((upper, lower)):
+            acc = jnp.dot(part, table[: part.shape[1]], preferred_element_type=F32)
+            rows = slice(b * BLOCK + i * half, b * BLOCK + (i + 1) * half)
+            out_ref[rows, :] = (acc[:, :128] / (acc[:, 128:129] + acc[:, 129:130])).astype(BF16)
 
 
 def layer_kernel(
@@ -239,20 +253,28 @@
     def load_queries():
         return pltpu.make_async_copy(q_hbm.at[0], kq, q_sem)
 
-    def load_centroids(h):
-        return pltpu.make_async_copy(cent_hbm.at[h], cents.at[h % 2], cent_sem.at[h % 2])
-
-    def store_out(h):
-        return pltpu.make_async_copy(outs.at[h % 2], out_hbm.at[0, :, lanes_of(h)], out_sem.at[h % 2])
-
-    def store_share(h):
-        return pltpu.make_async_copy(shares.at[h % 2], book_hbm.at[h], share_sem.at[h % 2])
+    def load_centroids(h, slot):
+        return pltpu.make_async_copy(cent_hbm.at[h], cents.at[slot], cent_sem.at[slot])
+
+    def store_out(h, slot):
+        return pltpu.make_async_copy(outs.at[slot], out_hbm.at[0, :, lanes_of(h)], out_sem.at[slot])
+
+    def store_share(h, slot):
+        return pltpu.make_async_copy(shares.at[slot], book_hbm.at[h], share_sem.at[slot])
 
     for g in range(GROUPS):
         load_keys(g).start()
         load_values(g).start()
     for h in range(2):
-        load_centroids(h).start()
+        load_centroids(h, h).start()
+
+    def sum_group(g):
+        load_keys(g).wait()
+        load_values(g).wait()
+        for i in range(PER_GROUP):
+            sum_head(
+                PER_GROUP * g + i, starts_ref, codes_ref, kq, values, kin, vin, early_sums, firsts
+            )
 
     barrier = pltpu.get_barrier_semaphore()
 
@@ -264,23 +286,16 @@
         greet(at(dx=k))
         greet(at(dz=k))
         greet(at_y(k))
+    sum_group(0)
     pl.semaphore_wait(barrier, 10)
 
     def share_cores(g):
         theirs = pl.ds(8 * g + 4 * (1 - c), 4)
+        remote(vin.at[theirs], vc.at[g], VAL_CORE, g, at(dc=1)).start()
         remote(kin.at[theirs], kc.at[g], KEY_CORE, g, at(dc=1)).start()
-        remote(vin.at[theirs], vc.at[g], VAL_CORE, g, at(dc=1)).start()
 
     def join(g):
         mine = 8 * g + 4 * c
-        arrived(KEY_CORE, g)
-
-        def add(u):
-            kc[g, u] = kc[g, u] + kin[mine + u]
-
-        unit_loop(add)
-        for k in (1, 2, 3):
-            remote(kc.at[g, (y + k) % 4], ky.at[g, 3 - k], KEY_Y, g, at_y(k)).start()
         arrived(VAL_CORE, g)
 
         def link(u):
@@ -294,6 +309,14 @@
         for k in (1, 2, 3):
             remote(vchip.at[g, (x + k) % 4], vx.at[g, x], VAL_X, g, at(dx=k)).start()
         vx[g, x] = vchip[g, x]
+        arrived(KEY_CORE, g)
+
+        def add(u):
+            kc[g, u] = kc[g, u] + kin[mine + u]
+
+        unit_loop(add)
+        for k in (1, 2, 3):
+            remote(kc.at[g, (y + k) % 4], ky.at[g, 3 - k], KEY_Y, g, at_y(k)).start()
 
     def keys_y(g):
         arrived(KEY_Y, g)
@@ -388,77 +411,68 @@
         remote(back.at[g], vout.at[pl.ds(mine, 4)], VAL_CB, g, at(dc=1)).start()
 
     def step(tick, carry):
-        @pl.when(tick < HEADS)
+        @pl.when((tick > 0) & (tick < GROUPS))
         def _():
-            h = tick
-            g = h // PER_GROUP
-
-            @pl.when(h % PER_GROUP == 0)
-            def _():
-                load_keys(g).wait()
-                load_values(g).wait()
-
-            sum_head(h, starts_ref, codes_ref, kq, values, kin, vin, early_sums, firsts)
-
-            @pl.when(h % PER_GROUP == PER_GROUP - 1)
-            def _():
-                share_cores(g)
-
-            @pl.when(h == HEADS - 1)
+            g = tick
+            sum_group(g)
+            share_cores(g)
+
+            @pl.when(g == GROUPS - 1)
             def _():
                 load_queries().start()
 
         @pl.when(tick >= ATTEND)
         def _():
-            h = tick - ATTEND
-            g = h // PER_GROUP
-
-            @pl.when(h == 0)
+            g = tick - ATTEND
+
+            @pl.when(g == 0)
             def _():
                 load_queries().wait()
 
-            @pl.when(h % PER_GROUP == 0)
+            @pl.when(g > 0)
             def _():
-                arrived(KEY_CB, g)
-                arrived(VAL_CB, g)
-
-            load_centroids(h).wait()
-
-            @pl.when(h >= 2)
+                for i in range(PER_GROUP):
+                    store_out(PER_GROUP * (g - 1) + i, i).wait()
+                    store_share(PER_GROUP * (g - 1) + i, i).wait()
+
+            for i in range(PER_GROUP):
+                load_centroids(PER_GROUP * g + i, i).wait()
+            arrived(KEY_CB, g)
+            arrived(VAL_CB, g)
+            for i in range(PER_GROUP):
+                attend_head(
+                    PER_GROUP * g + i, y, starts_ref, codes_ref, old_ref, kq, values, kout, vout,
+                    early_sums, firsts, cents.at[i], book_ref.at[i], outs.at[i], shares.at[i],
+                )
+            for i in range(PER_GROUP):
+                store_out(PER_GROUP * g + i, i).start()
+                store_share(PER_GROUP * g + i, i).start()
+
+            @pl.when(g + 1 < GROUPS)
             def _():
-                store_out(h - 2).wait()
-                store_share(h - 2).wait()
-
-            attend_head(
-                h, y, starts_ref, codes_ref, old_ref, kq, values, kout, vout, early_sums, firsts,
-                cents.at[h % 2], book_ref, outs.at[h % 2], shares.at[h % 2],
-            )
-            store_out(h).start()
-            store_share(h).start()
-
-            @pl.when(h + 2 < HEADS)
-            def _():
-                load_centroids(h + 2).start()
+                for i in range(PER_GROUP):
+                    load_centroids(PER_GROUP * (g + 1) + i, i).start()
 
         for when, stage in (
             (AT_YB, keys_back_y), (AT_SPLIT, split), (AT_ZB, keys_back_z), (AT_X, keys_x),
             (AT_Z, keys_z), (AT_ROWS, scan_rows), (AT_Y, keys_y), (AT_SCAN, scan_row),
             (AT_JOIN, join),
         ):
-            first, stride = when
-            since = tick - first
-
-            @pl.when((since >= 0) & (since % stride == 0) & (since < GROUPS * stride))
-            def _(stage=stage, since=since, stride=stride):
-                stage(since // stride)
+
+            def one(g, carry, stage=stage):
+                stage(g)
+                return carry
+
+            lax.fori_loop(groups_before(when, tick), groups_before(when, tick + 1), one, 0)
 
         return carry
 
-    lax.fori_loop(0, ATTEND + HEADS, step, 0)
-
-    for h in (HEADS - 2, HEADS - 1):
-        store_out(h).wait()
-        store_share(h).wait()
+    share_cores(0)
+    lax.fori_loop(1, ATTEND + GROUPS, step, 0)
+
+    for i in range(PER_GROUP):
+        store_out(HEADS - PER_GROUP + i, i).wait()
+        store_share(HEADS - PER_GROUP + i, i).wait()
 
     def finish(g, carry):
         for phase in range(PHASES):
@@ -488,7 +502,7 @@
             pltpu.VMEM((TOK_DEV, HEADS * HEAD_DIM), BF16),
             pltpu.VMEM((TOK_DEV, HEADS * HEAD_DIM), BF16),
             units(2, CODES),
-            units(CODES),
+            units(2, CODES),
             pltpu.VMEM((2, TOK_DEV, HEAD_DIM), BF16),
             units(2, CODES // 4),
             pltpu.VMEM((HEADS, 8, CODES), F32),
@@ -525,8 +539,45 @@
     )(starts, codes, old, queries, keys, values, centroids)
 
 
+def deliver_kernel(out_hbm, book_hbm, out_to, book_to, rows_held, book_held, sems):
+    pieces = []
+    for i in range(8):
+        rows = pl.ds(i * 128, 128)
+        pieces.append((out_hbm.at[0, rows], rows_held.at[rows], out_to.at[0, rows]))
+    pieces.append((book_hbm, book_held, book_to))
+    inward = [pltpu.make_async_copy(a, b, sems.at[0, i]) for i, (a, b, c) in enumerate(pieces)]
+    outward = [pltpu.make_async_copy(b, c, sems.at[1, i]) for i, (a, b, c) in enumerate(pieces)]
+    for copy in inward:
+        copy.start()
+    for arriving, leaving in zip(inward, outward):
+        arriving.wait()
+        leaving.start()
+    for copy in outward:
+        copy.wait()
+
+
+def deliver(out, book):
+    hbm = pl.BlockSpec(memory_space=pltpu.HBM)
+    return pl.pallas_call(
+        deliver_kernel,
+        name="deliver",
+        out_shape=(
+            jax.ShapeDtypeStruct(out.shape, out.dtype),
+            jax.ShapeDtypeStruct(book.shape, book.dtype),
+        ),
+        in_specs=[hbm, hbm],
+        out_specs=[hbm, hbm],
+        scratch_shapes=[
+            pltpu.VMEM(out.shape[1:], out.dtype),
+            pltpu.VMEM(book.shape, book.dtype),
+            pltpu.SemaphoreType.DMA((2, 9)),
+        ],
+        compiler_params=pltpu.CompilerParams(vmem_limit_bytes=60 << 20),
+    )(out, book)
+
+
 def shards(queries, keys, values, codes, starts, old_centroids, old_counts):
-    return layer(queries, keys, values, codes, starts, old_centroids, old_counts)
+    return deliver(*layer(queries, keys, values, codes, starts, old_centroids, old_counts))
 
 
 def solution(mesh):

time: 96.2 us -> 92.8 us (0.965)
  local copies, waits for them, and re-layouts: 5.85 us -> 0 us
  Pallas kernels: 89.4 us -> 92 us
    unnamed x4 -> x0, local copies, waits for them, and re-layouts: 5.85 us -> none
    pallas_call x0 -> x1, Pallas kernels: none -> 4.9 us  [deliver(): pl.pallas_call(deliver_kernel, name='deliver', out_shape=(jax.ShapeDtypeS...]
    pallas_call x1, Pallas kernels: 89.4 us -> 87.1 us  [layer(): pl.pallas_call(layer_kernel, name='layer', out_shape=(jax.ShapeDtypeStruc...]
where the time goes in v5:
time: 92.8 us; the launch traced here: 92.6 us
  Pallas kernels  92 us (99%)
    pallas_call x1, Pallas kernels, layer(): pl.pallas_call(layer_kernel, name='layer', out_shape=(jax.ShapeDtypeStruc...  87.1 us
    pallas_call x1, Pallas kernels, deliver(): pl.pallas_call(deliver_kernel, name='deliver', out_shape=(jax.ShapeDtypeS...  4.9 us

profile of v5, /device:TPU:0, one launch (start us, length us, event | category | flops | bytes accessed | tf_op | source)
XLA Modules:
  0.0 92.6 jit_solution(12418973681185804973)
XLA Ops:
  0.6 87.1 %layer.1 = (bf16[1,1024,2048]{2,1,0:T(8,128)(2,1)}, f32[16,128,128]{2,1,0:T(8,128)}) custom-call(s32[1,2]{1,0:T(1,128)} %starts_ref.1, s32[1,16,1024]{2,1,0:T(8,128)} %codes_ref.1, f32[16,512]{1,0:T(8,128)} %old_ref.1, bf16[1,1024,2048]{2,1,0:T(8,128)(2,1)} %q_hbm.1, bf16[1,1024,2048]{2,1,0:T(8,128)(2,1)} %k_hbm.1, bf16[1,1024,2048]{2,1,0:T(8,128)(2,1)} %v_hbm.1, ...), custom_call_target="tpu_custom_call" | custom-call | tf_op jit(solution)/shard_map/layer/pallas_call | solution.py:492
  87.7 4.9 %deliver.1 = (bf16[1,1024,2048]{2,1,0:T(8,128)(2,1)}, f32[16,128,128]{2,1,0:T(8,128)}) custom-call(bf16[1,1024,2048]{2,1,0:T(8,128)(2,1)} %get-tuple-element.4.out_hbm, f32[16,128,128]{2,1,0:T(8,128)} %get-tuple-element.5.book_hbm), custom_call_target="tpu_custom_call" | custom-call | tf_op jit(solution)/shard_map/deliver/pallas_call | solution.py:561

commit v6 on v5

--- a/solution.py
+++ b/solution.py
@@ -30,13 +30,13 @@
 ATTEND = 9
 AT_JOIN = (1, 2, 3, 4, 5, 6, 7, 8)
 AT_Y = (3, 4, 5, 6, 6, 7, 8, 9)
-AT_SCAN = (3, 4, 5, 7, 7, 8, 10, 10)
+AT_SCAN = (3, 4, 5, 6, 7, 8, 9, 10)
 AT_Z = (4, 5, 6, 7, 7, 8, 10, 10)
-AT_ROWS = (5, 6, 7, 8, 9, 10, 11, 12)
+AT_ROWS = (5, 6, 7, 8, 9, 10, 11, 11)
 AT_X = (5, 6, 7, 8, 8, 10, 11, 11)
 AT_ZB = (6, 7, 8, 9, 9, 11, 12, 12)
-AT_SPLIT = (7, 8, 9, 10, 11, 12, 13, 14)
-AT_YB = (7, 8, 9, 10, 11, 12, 13, 14)
+AT_SPLIT = (7, 8, 9, 10, 11, 12, 12, 13)
+AT_YB = (7, 8, 9, 10, 11, 12, 13, 13)
 
 
 def groups_before(when, tick):

time: 92.8 us -> 93.9 us (1.012)
  Pallas kernels: 92 us -> 93.1 us
    pallas_call x1, Pallas kernels: 87.1 us -> 88.2 us  [layer(): pl.pallas_call(layer_kernel, name='layer', out_shape=(jax.ShapeDtypeStruc...]
where the time goes in v6:
time: 93.9 us; the launch traced here: 93.8 us
  Pallas kernels  93.1 us (99%)
    pallas_call x1, Pallas kernels, layer(): pl.pallas_call(layer_kernel, name='layer', out_shape=(jax.ShapeDtypeStruc...  88.2 us
    pallas_call x1, Pallas kernels, deliver(): pl.pallas_call(deliver_kernel, name='deliver', out_shape=(jax.ShapeDtypeS...  4.9 us

profile of v6, /device:TPU:0, one launch (start us, length us, event | category | flops | bytes accessed | tf_op | source)
XLA Modules:
  0.0 93.8 jit_solution(11246680411674955136)
XLA Ops:
  0.6 88.2 %layer.1 = (bf16[1,1024,2048]{2,1,0:T(8,128)(2,1)}, f32[16,128,128]{2,1,0:T(8,128)}) custom-call(s32[1,2]{1,0:T(1,128)} %starts_ref.1, s32[1,16,1024]{2,1,0:T(8,128)} %codes_ref.1, f32[16,512]{1,0:T(8,128)} %old_ref.1, bf16[1,1024,2048]{2,1,0:T(8,128)(2,1)} %q_hbm.1, bf16[1,1024,2048]{2,1,0:T(8,128)(2,1)} %k_hbm.1, bf16[1,1024,2048]{2,1,0:T(8,128)(2,1)} %v_hbm.1, ...), custom_call_target="tpu_custom_call" | custom-call | tf_op jit(solution)/shard_map/layer/pallas_call | solution.py:492
  88.9 4.9 %deliver.1 = (bf16[1,1024,2048]{2,1,0:T(8,128)(2,1)}, f32[16,128,128]{2,1,0:T(8,128)}) custom-call(bf16[1,1024,2048]{2,1,0:T(8,128)(2,1)} %get-tuple-element.4.out_hbm, f32[16,128,128]{2,1,0:T(8,128)} %get-tuple-element.5.book_hbm), custom_call_target="tpu_custom_call" | custom-call | tf_op jit(solution)/shard_map/deliver/pallas_call | solution.py:561
